TPU v7x, 256 devices: a whole 4x4x8 slice. The times are simulated.
256 devices in a mesh: req: 64 (over z, x, core), tp: 4 (over y).
Axes of the slice: x: 4, y: 4, z: 8, core: 2. Of those that a mesh axis runs over, the one named last changes fastest.
Arguments:
- hidden_in: bfloat16 [32768, 1024], P('req', 'tp'), may hold values from -6 to 6
- w_qkv: bfloat16 [1024, 3, 1024], P(None, None, 'tp'), may hold values from -0.1875 to 0.1875
- w_out: bfloat16 [1024, 1024], P('tp'), may hold values from -0.75 to 0.75
- first_gain: float32 [1024], replicated, may hold values from 0.1 to 1.9
- w_up: bfloat16 [1024, 4096], P(None, 'tp'), may hold values from -0.1875 to 0.1875
- w_down: bfloat16 [4096, 1024], P('tp'), may hold values from -0.09375 to 0.09375
- second_gain: float32 [1024], replicated, may hold values from 0.1 to 1.9
- cache_pool: bfloat16 [4096, 128, 2, 1024], P('req', None, None, 'tp'), may hold values from -600 to 600
- page_table: int32 [512, 8], P('req'), may hold values from 0 to 63, as said below
- cache_len: int32 [512], P('req'), may hold values from 1 to 1024, as said below
- tree_parent: int32 [512, 64], P('req'), may hold values from -1 to 62, as said below
- accept_node: int32 [512], P('req'), may hold values from 0 to 63
Outputs:
- layer_out: bfloat16 [32768, 1024], P('req', 'tp')
- accepted_kv: bfloat16 [512, 64, 2, 1024], P('req', None, None, 'tp')
Inputs may be any that keep to these rules, and one draw needn't show every extreme that they name: `page_table`: on each index e of req, the 8 x 8 entries of its rows are a permutation of the slots 0 to 63; row j, column m holds the slot in e's pool of page j of member m of the index e - j of req (modulo the axis size). `cache_len`: on each index of req exactly 2 requests have lengths over 256, and the others at most 256; the length 1024 occurs in every draw, and so does the length 256. `tree_parent`: node 0 is the root with parent -1; every other node's parent is an earlier node.
All inputs are finite; a program needn't handle non-finite values.
Results may differ from a plain program's by a relative error of at most 0.012.
Values may be sent and summed in bfloat16 or wider, within the bound.
A program may use at most 128 MiB of HBM per device.

v0:
```python
import jax
import jax.numpy as jnp
from jax import lax
from jax.sharding import PartitionSpec as P

HD = 64


NEG = -1e30
EPS = 1e-05


def from_behind(value, axis, by):
    size = lax.axis_size(axis)
    return lax.ppermute(value, axis, [(i, (i + by) % size) for i in range(size)])


def block_partial(queries, key_rows, value_rows, valid):
    scores = jnp.einsum("bqhd,bkhd->bhqk", queries, key_rows, preferred_element_type=jnp.float32)
    allowed = valid[:, None, :, :]
    maxima = jnp.max(jnp.where(allowed, scores, NEG), axis=-1)
    weights = jnp.where(allowed, jnp.exp(scores - maxima[..., None]), 0.0).astype(jnp.bfloat16)
    totals = jnp.sum(weights.astype(jnp.float32), axis=-1)
    mixture = jnp.einsum("bhqk,bkhd->bqhd", weights, value_rows, preferred_element_type=jnp.float32)
    return (mixture, maxima, totals)


def combine_blocks(mixture, maxima, totals):
    best = jnp.max(maxima, axis=0)
    scale = jnp.swapaxes(jnp.exp(maxima - best[None]), -1, -2)
    numer = jnp.sum(mixture * scale[..., None], axis=0)
    denom = jnp.sum(jnp.swapaxes(totals, -1, -2) * scale, axis=0)
    return numer / denom[..., None]


def ancestors(parents):
    count = parents.shape[-1]
    reach = jax.nn.one_hot(parents, count, dtype=jnp.float32) + jnp.eye(count, dtype=jnp.float32)
    for sweep in range(max(1, (count - 1).bit_length())):
        reach = jnp.minimum(
            jnp.einsum("rij,rjk->rik", reach, reach, precision=lax.Precision.HIGHEST), 1.0
        )
    return reach


def page_rows(cache_pool, slot_ids):
    picker = jax.nn.one_hot(slot_ids, cache_pool.shape[0], dtype=jnp.bfloat16)
    return jnp.einsum(
        "rs,spcf->rpcf", picker, cache_pool, preferred_element_type=jnp.float32
    ).astype(jnp.bfloat16)


def rows_split(rows, heads_local):
    requests, page_len = (rows.shape[0], rows.shape[1])
    return (
        rows[:, :, 0].reshape(requests, page_len, heads_local, HD),
        rows[:, :, 1].reshape(requests, page_len, heads_local, HD),
    )


def page_split(cache_pool, slot_ids, heads_local):
    return rows_split(page_rows(cache_pool, slot_ids), heads_local)


def spread_back(arrived, long_ids, requests):
    mixture = (
        jnp.zeros((requests,) + arrived[0].shape[1:], jnp.float32).at[long_ids].set(arrived[0])
    )
    maxima = (
        jnp.full((requests,) + arrived[1].shape[1:], NEG, jnp.float32).at[long_ids].set(arrived[1])
    )
    totals = jnp.zeros((requests,) + arrived[2].shape[1:], jnp.float32).at[long_ids].set(arrived[2])
    return (mixture, maxima, totals)


def norm_from_sums(values, sums, gain, width_all):
    center = (sums[0] / width_all)[:, None]
    spread = (sums[1] / width_all)[:, None] - center * center
    return (values - center) * lax.rsqrt(spread + EPS) * gain


def shards(
    hidden_in,
    w_qkv,
    w_out,
    first_gain,
    w_up,
    w_down,
    second_gain,
    cache_pool,
    page_table,
    cache_len,
    tree_parent,
    accept_node,
):
    tokens_dev, share = hidden_in.shape
    requests, draft = tree_parent.shape
    width_local = w_qkv.shape[2]
    heads_local = width_local // HD
    page_count = page_table.shape[0]
    page_len = cache_pool.shape[1]
    width_all = share * lax.axis_size("tp")
    start = lax.axis_index("tp") * share
    gathered = lax.all_gather(hidden_in, "tp", axis=1, tiled=True)
    projected = jnp.einsum("td,dcf->tcf", gathered, w_qkv, preferred_element_type=jnp.float32)
    queries = (
        (projected[:, 0] * 0.125).astype(jnp.bfloat16).reshape(requests, draft, heads_local, HD)
    )
    key_new = projected[:, 1].astype(jnp.bfloat16)
    value_new = projected[:, 2].astype(jnp.bfloat16)
    key_heads = key_new.reshape(requests, draft, heads_local, HD)
    value_heads = value_new.reshape(requests, draft, heads_local, HD)
    reach = ancestors(tree_parent)
    long_count = (requests + 3) // 4
    is_long = (cache_len > 2 * page_len).astype(jnp.int32)
    rank_score = is_long * (2 * requests) + (requests - jnp.arange(requests, dtype=jnp.int32))
    ranked, long_ids = lax.top_k(rank_score, long_count)
    long_queries = queries[long_ids]
    member_code = long_ids.astype(jnp.bfloat16)
    parts = [block_partial(queries, key_heads, value_heads, reach > 0.5)]
    positions = jnp.arange(page_len, dtype=jnp.int32)
    for page_index in range(page_count):
        valid_rows = page_index * page_len + positions[None, :] < cache_len[:, None]
        valid = jnp.broadcast_to(valid_rows[:, None, :], (requests, draft, page_len))
        if page_index == 0:
            key_rows, value_rows = page_split(cache_pool, page_table[0], heads_local)
            result = block_partial(queries, key_rows, value_rows, valid)
        elif page_index == 1:
            incoming, flags = from_behind(
                (queries, valid_rows.astype(jnp.bfloat16)), "req", page_index
            )
            key_rows, value_rows = page_split(cache_pool, page_table[page_index], heads_local)
            remote_valid = jnp.broadcast_to((flags > 0.5)[:, None, :], (requests, draft, page_len))
            remote = block_partial(incoming, key_rows, value_rows, remote_valid)
            result = from_behind((remote[0], remote[1], remote[2]), "req", -page_index)
        else:
            long_flags = valid_rows[long_ids].astype(jnp.bfloat16)
            incoming, flags, members = from_behind(
                (long_queries, long_flags, member_code), "req", page_index
            )
            member_ids = members.astype(jnp.int32)
            key_rows, value_rows = page_split(
                cache_pool, page_table[page_index][member_ids], heads_local
            )
            remote_valid = jnp.broadcast_to(
                (flags > 0.5)[:, None, :], (long_count, draft, page_len)
            )
            remote = block_partial(incoming, key_rows, value_rows, remote_valid)
            arrived = from_behind((remote[0], remote[1], remote[2]), "req", -page_index)
            result = spread_back(arrived, long_ids, requests)
        parts.append(result)
    mixture = jnp.stack([piece[0] for piece in parts], axis=0)
    maxima = jnp.stack([piece[1] for piece in parts], axis=0)
    totals = jnp.stack([piece[2] for piece in parts], axis=0)
    attended = (
        combine_blocks(mixture, maxima, totals)
        .reshape(tokens_dev, width_local)
        .astype(jnp.bfloat16)
    )
    branch = jnp.dot(attended, w_out, preferred_element_type=jnp.float32)
    second_share = lax.dynamic_slice_in_dim(second_gain, start, share, 0)
    summed = lax.psum(branch, "tp")
    mixed_all = gathered.astype(jnp.float32) + summed
    whole_sums = (jnp.sum(mixed_all, axis=-1), jnp.sum(mixed_all * mixed_all, axis=-1))
    normed_all = norm_from_sums(mixed_all, whole_sums, first_gain, width_all).astype(jnp.bfloat16)
    normed_share = lax.dynamic_slice_in_dim(normed_all, start, share, 1)
    inner = jax.nn.gelu(
        jnp.dot(normed_all, w_up, preferred_element_type=jnp.float32), approximate=False
    ).astype(jnp.bfloat16)
    outer = lax.psum_scatter(
        jnp.dot(inner, w_down, preferred_element_type=jnp.float32).astype(jnp.bfloat16),
        "tp",
        scatter_dimension=1,
        tiled=True,
    ).astype(jnp.float32)
    second_in = normed_share.astype(jnp.float32) + outer
    second_sums = lax.psum(
        (jnp.sum(second_in, axis=-1), jnp.sum(second_in * second_in, axis=-1)), "tp"
    )
    layer_out = norm_from_sums(second_in, second_sums, second_share, width_all).astype(jnp.bfloat16)
    pairs = jnp.stack(
        [
            key_new.reshape(requests, draft, width_local),
            value_new.reshape(requests, draft, width_local),
        ],
        axis=2,
    )
    depth = jnp.sum(reach, axis=-1) - 1.0
    chosen = jnp.einsum(
        "rq,rqk->rk",
        jax.nn.one_hot(accept_node, draft, dtype=jnp.float32),
        reach,
        precision=lax.Precision.HIGHEST,
    )
    levels = jnp.arange(draft, dtype=jnp.float32)
    select = (
        chosen[:, None, :] * (depth[:, None, :] == levels[None, :, None]).astype(jnp.float32)
    ).astype(jnp.bfloat16)
    accepted_kv = jnp.einsum(
        "rsk,rkcf->rscf", select, pairs, preferred_element_type=jnp.float32
    ).astype(jnp.bfloat16)
    return (layer_out, accepted_kv)


def solution(mesh):
    placed = (
        P("req", "tp"),
        P(None, None, "tp"),
        P("tp", None),
        P(),
        P(None, "tp"),
        P("tp", None),
        P(),
        P("req", None, None, "tp"),
        P("req", None),
        P("req"),
        P("req", None),
        P("req"),
    )
    return jax.shard_map(
        shards,
        mesh=mesh,
        in_specs=placed,
        out_specs=(P("req", "tp"), P("req", None, None, "tp")),
        check_vma=False,
    )
```

profile of v0, /device:TPU:2, one launch (start us, length us, event | category | flops | bytes accessed | tf_op | source)
XLA Modules:
  0.0 424.8 jit_solution(16485412989436485535)
XLA Ops:
  11.1 4.3 %collective-permute-start.15 = (bf16[2]{0:T(256)(128)(2,1)S(1)}, bf16[2]{0:T(256)(128)(2,1)S(1)}, u32[]{:S(2)}, u32[]{:S(2)}) collective-permute-start(bf16[2]{0:T(256)(128)(2,1)S(1)} %get-tuple-element.60), channel_id=1, source_target_pairs={{0,20},{4,24},{8,28},{12,32},{16,36},{20,40},{24,44},{28,48},{32,5... | collective-permute-start | bytes 20 | tf_op jit(solution)/shard_map/ppermute | solution.py:15
  21.2 7.9 %convolution_convert_fusion.2 = bf16[8,128,2,256]{3,0,2,1:T(8,128)(2,1)S(1)} fusion(bf16[64,128,2,256]{3,2,1,0:T(2,128)(2,1)} %param.19, s32[8]{0:T(128)S(1)} %get-tuple-element.46), kind=kOutput, calls=%fused_computation.56 | convolution fusion | flops 67633664 | bytes 9437216 | tf_op jit(solution)/shard_map/rs,spcf->rpcf/dot_general | solution.py:48
  33.9 8.4 %convolution_convert_fusion.1 = bf16[8,128,2,256]{3,0,2,1:T(8,128)(2,1)S(1)} fusion(bf16[64,128,2,256]{3,2,1,0:T(2,128)(2,1)} %param.19, s32[8]{0:T(128)S(1)} %get-tuple-element.45), kind=kOutput, calls=%fused_computation.55 | convolution fusion | flops 67633664 | bytes 9437216 | tf_op jit(solution)/shard_map/rs,spcf->rpcf/dot_general | solution.py:48
  55.3 8.0 %fusion.26 = bf16[2,128,2,256]{3,0,2,1:T(2,128)(2,1)S(1)} fusion(bf16[64,128,2,256]{3,2,1,0:T(2,128)(2,1)} %param.19, s32[2]{0:T(128)S(1)} %gather_fusion), kind=kOutput, calls=%fused_computation.77 | convolution fusion | flops 16908416 | bytes 8650760 | tf_op jit(solution)/shard_map/rs,spcf->rpcf/dot_general | solution.py:48
  64.8 8.0 %fusion.29 = bf16[2,128,2,256]{3,0,2,1:T(2,128)(2,1)S(1)} fusion(bf16[64,128,2,256]{3,2,1,0:T(2,128)(2,1)} %param.19, s32[2]{0:T(128)S(1)} %gather_fusion.3), kind=kOutput, calls=%fused_computation.78 | convolution fusion | flops 16908416 | bytes 8650760 | tf_op jit(solution)/shard_map/rs,spcf->rpcf/dot_general | solution.py:48
  76.1 3.1 collective-permute-start.8
  79.9 8.0 %fusion.32 = bf16[2,128,2,256]{3,0,2,1:T(2,128)(2,1)S(1)} fusion(bf16[64,128,2,256]{3,2,1,0:T(2,128)(2,1)} %param.19, s32[2]{0:T(128)S(1)} %gather_fusion.5), kind=kOutput, calls=%fused_computation.79 | convolution fusion | flops 16908416 | bytes 8650760 | tf_op jit(solution)/shard_map/rs,spcf->rpcf/dot_general | solution.py:48
  89.4 8.0 %fusion.35 = bf16[2,128,2,256]{3,0,2,1:T(2,128)(2,1)S(1)} fusion(bf16[64,128,2,256]{3,2,1,0:T(2,128)(2,1)} %param.19, s32[2]{0:T(128)S(1)} %gather_fusion.7), kind=kOutput, calls=%fused_computation.80 | convolution fusion | flops 16908416 | bytes 8650760 | tf_op jit(solution)/shard_map/rs,spcf->rpcf/dot_general | solution.py:48
  100.4 3.7 collective-permute-start.16
  104.7 8.0 %fusion.38 = bf16[2,128,2,256]{3,0,2,1:T(2,128)(2,1)S(1)} fusion(bf16[64,128,2,256]{3,2,1,0:T(2,128)(2,1)} %param.19, s32[2]{0:T(128)S(1)} %gather_fusion.9), kind=kOutput, calls=%fused_computation.81 | convolution fusion | flops 16908416 | bytes 8650760 | tf_op jit(solution)/shard_map/rs,spcf->rpcf/dot_general | solution.py:48
  114.2 8.0 %fusion.41 = bf16[2,128,2,256]{3,0,2,1:T(2,128)(2,1)S(1)} fusion(bf16[64,128,2,256]{3,2,1,0:T(2,128)(2,1)} %param.19, s32[2]{0:T(128)S(1)} %gather_fusion.11), kind=kOutput, calls=%fused_computation.82 | convolution fusion | flops 16908416 | bytes 8650760 | tf_op jit(solution)/shard_map/rs,spcf->rpcf/dot_general | solution.py:48
  140.7 3.8 collective-permute-done.20
  193.5 4.2 collective-permute-start.29
  198.5 4.0 collective-permute-start.40
  204.2 3.1 collective-permute-start.32
  213.4 4.9 %collective-permute-done.6 = f32[2,64,4,64]{1,3,2,0:T(8,128)S(1)} collective-permute-done((f32[2,64,4,64]{1,3,2,0:T(8,128)S(1)}, f32[2,64,4,64]{1,3,2,0:T(8,128)S(1)}, u32[]{:S(2)}, u32[]{:S(2)}) %collective-permute-start.6) | collective-permute-done | bytes 131104 | tf_op jit(solution)/shard_map/ppermute | solution.py:15
  218.3 4.8 %collective-permute-start.22 = (f32[2,64,4,64]{1,3,2,0:T(8,128)}, f32[2,64,4,64]{1,3,2,0:T(8,128)}, u32[]{:S(2)}, u32[]{:S(2)}) collective-permute-start(f32[2,64,4,64]{1,3,2,0:T(8,128)} %convolution_bitcast_fusion.4), channel_id=1, source_target_pairs={{0,232},{4,236},{8,240},{12,244},{16,248},{20,252},{24,0},{28,4},{... | collective-permute-start | bytes 393224 | tf_op jit(solution)/shard_map/ppermute | solution.py:15
  265.7 4.7 %collective-permute-start.2 = (f32[8,64,4,64]{1,3,2,0:T(8,128)S(1)}, f32[8,64,4,64]{1,3,2,0:T(8,128)S(1)}, u32[]{:S(2)}, u32[]{:S(2)}) collective-permute-start(f32[8,64,4,64]{1,3,2,0:T(8,128)S(1)} %convolution_bitcast_fusion), channel_id=1, source_target_pairs={{0,252},{4,0},{8,4},{12,8},{16,12},{20,16},{24,20},{28,24},{32,28}... | collective-permute-start | bytes 1572872 | tf_op jit(solution)/shard_map/ppermute | solution.py:15
  275.7 7.0 %collective-permute-done.2 = f32[8,64,4,64]{1,3,2,0:T(8,128)S(1)} collective-permute-done((f32[8,64,4,64]{1,3,2,0:T(8,128)S(1)}, f32[8,64,4,64]{1,3,2,0:T(8,128)S(1)}, u32[]{:S(2)}, u32[]{:S(2)}) %collective-permute-start.2) | collective-permute-done | bytes 524320 | tf_op jit(solution)/shard_map/ppermute | solution.py:15
  290.5 5.6 %multiply_reduce_fusion = f32[8,64,4,64]{1,3,2,0:T(8,128)S(1)} fusion(f32[9,8,64,4,64]{2,4,3,1,0:T(8,128)} %bitcast_dynamic-update-slice_fusion, f32[9,8,64,4]{2,3,1,0:T(4,128)S(1)} %get-tuple-element.21), kind=kLoop, calls=%fused_computation.31 | loop fusion | flops 2228224 | bytes 5316608 | tf_op jit(solution)/shard_map/reduce_sum | solution.py:31
  300.6 66.8 %all-reduce.3.cloned.1.call-done = f32[512,1024]{1,0:T(8,128)} async-done(((f32[512,1024]{1,0:T(8,128)}), f32[512,1024]{1,0:T(8,128)}) %all-reduce.3.cloned.1.call-update) | async-done | bytes 2097168 | tf_op jit(solution)/shard_map/psum | solution.py:162
  371.1 9.2 %convolution_convert_fusion = bf16[512,1024]{1,0:T(8,128)(2,1)} fusion(bf16[1024,1024]{1,0:T(8,128)(2,1)S(1)} %copy-done, bf16[512,1024]{1,0:T(8,128)(2,1)} %multiply_convert_fusion, bf16[1024,1024]{1,0:T(8,128)(2,1)} %param.16), kind=kOutput, calls=%fused_computation.54 | convolution fusion | flops 2182086656 | bytes 6291456 | tf_op jit(solution)/shard_map/dot_general | solution.py:171
  384.2 22.1 %reduce-scatter.2.cloned.1.call-done = bf16[512,256]{1,0:T(8,128)(2,1)} async-done(((bf16[512,1024]{1,0:T(8,128)(2,1)}), bf16[512,256]{1,0:T(8,128)(2,1)}) %reduce-scatter.2.cloned.1.call-update) | async-done | bytes 262160 | tf_op jit(solution)/shard_map/reduce_scatter | solution.py:170
  407.5 8.5 %all-reduce = (f32[512]{0:T(512)S(1)}, f32[512]{0:T(512)S(1)}) all-reduce(f32[512]{0:T(512)S(1)} %get-tuple-element.17, f32[512]{0:T(512)S(1)} %get-tuple-element.16), channel_id=1, replica_groups=mesh['req'=64,'tp'=4] {'tp'}, use_global_device_ids=true, to_apply=%region_46.47 | all-reduce | flops 1024 | bytes 8192 | tf_op jit(solution)/shard_map/psum | solution.py:177
  (378 shorter events, 185.8 us)
Async XLA Ops:
  7.2 137.3 %all-gather.2.cloned.1.call-start = ((), (), s32[]{:S(2)}) async-start(), calls=%async_computation.1 | async-start | bytes 1310720 | tf_op jit(solution)/shard_map/all_gather | solution.py:104
  9.0 42.3 %collective-permute-start.7 = (bf16[2]{0:T(256)(128)(2,1)S(1)}, bf16[2]{0:T(256)(128)(2,1)S(1)}, u32[]{:S(2)}, u32[]{:S(2)}) collective-permute-start(bf16[2]{0:T(256)(128)(2,1)S(1)} %get-tuple-element.60), channel_id=1, source_target_pairs={{0,12},{4,16},{8,20},{12,24},{16,28},{20,32},{24,36},{28,40},{32,4... | collective-permute-start | bytes 20 | tf_op jit(solution)/shard_map/ppermute | solution.py:15
  9.9 44.3 %collective-permute-start.3 = (bf16[2]{0:T(256)(128)(2,1)S(1)}, bf16[2]{0:T(256)(128)(2,1)S(1)}, u32[]{:S(2)}, u32[]{:S(2)}) collective-permute-start(bf16[2]{0:T(256)(128)(2,1)S(1)} %get-tuple-element.60), channel_id=1, source_target_pairs={{0,8},{4,12},{8,16},{12,20},{16,24},{20,28},{24,32},{28,36},{32,40... | collective-permute-start | bytes 20 | tf_op jit(solution)/shard_map/ppermute | solution.py:15
  11.1 62.6 %collective-permute-start.15 = (bf16[2]{0:T(256)(128)(2,1)S(1)}, bf16[2]{0:T(256)(128)(2,1)S(1)}, u32[]{:S(2)}, u32[]{:S(2)}) collective-permute-start(bf16[2]{0:T(256)(128)(2,1)S(1)} %get-tuple-element.60), channel_id=1, source_target_pairs={{0,20},{4,24},{8,28},{12,32},{16,36},{20,40},{24,44},{28,48},{32,5... | collective-permute-start | bytes 20 | tf_op jit(solution)/shard_map/ppermute | solution.py:15
  15.4 60.7 %collective-permute-start.11 = (bf16[2]{0:T(256)(128)(2,1)S(1)}, bf16[2]{0:T(256)(128)(2,1)S(1)}, u32[]{:S(2)}, u32[]{:S(2)}) collective-permute-start(bf16[2]{0:T(256)(128)(2,1)S(1)} %get-tuple-element.60), channel_id=1, source_target_pairs={{0,16},{4,20},{8,24},{12,28},{16,32},{20,36},{24,40},{28,44},{32,4... | collective-permute-start | bytes 20 | tf_op jit(solution)/shard_map/ppermute | solution.py:15
  16.7 81.7 %collective-permute-start.23 = (bf16[2]{0:T(256)(128)(2,1)S(1)}, bf16[2]{0:T(256)(128)(2,1)S(1)}, u32[]{:S(2)}, u32[]{:S(2)}) collective-permute-start(bf16[2]{0:T(256)(128)(2,1)S(1)} %get-tuple-element.60), channel_id=1, source_target_pairs={{0,28},{4,32},{8,36},{12,40},{16,44},{20,48},{24,52},{28,56},{32,6... | collective-permute-start | bytes 20 | tf_op jit(solution)/shard_map/ppermute | solution.py:15
  17.4 350.0 %all-reduce.3.cloned.1.call-start = ((), (), s32[]{:S(2)}) async-start(), calls=%async_computation.2 | async-start | bytes 4194304 | tf_op jit(solution)/shard_map/psum | solution.py:162
  51.3 49.1 %collective-permute-start.19 = (bf16[2]{0:T(256)(128)(2,1)S(1)}, bf16[2]{0:T(256)(128)(2,1)S(1)}, u32[]{:S(2)}, u32[]{:S(2)}) collective-permute-start(bf16[2]{0:T(256)(128)(2,1)S(1)} %get-tuple-element.60), channel_id=1, source_target_pairs={{0,24},{4,28},{8,32},{12,36},{16,40},{20,44},{24,48},{28,52},{32,5... | collective-permute-start | bytes 20 | tf_op jit(solution)/shard_map/ppermute | solution.py:15
  54.2 90.3 %collective-permute-start = (bf16[8,128]{1,0:T(8,128)(2,1)S(1)}, bf16[8,128]{1,0:T(8,128)(2,1)S(1)}, u32[]{:S(2)}, u32[]{:S(2)}) collective-permute-start(bf16[8,128]{1,0:T(8,128)(2,1)S(1)} %get-tuple-element.53), channel_id=1, source_target_pairs={{0,4},{4,8},{8,12},{12,16},{16,20},{20,24},{24,28},{28,32},{32,36}... | collective-permute-start | bytes 6152 | tf_op jit(solution)/shard_map/ppermute | solution.py:15
  73.7 65.1 %collective-permute-start.4 = (bf16[2,128]{1,0:T(2,128)(2,1)S(1)}, bf16[2,128]{1,0:T(2,128)(2,1)S(1)}, u32[]{:S(2)}, u32[]{:S(2)}) collective-permute-start(bf16[2,128]{1,0:T(2,128)(2,1)S(1)} %convert_element_type.237), channel_id=1, source_target_pairs={{0,8},{4,12},{8,16},{12,20},{16,24},{20,28},{24,32},{28,36},{32,40... | collective-permute-start | bytes 1544 | tf_op jit(solution)/shard_map/ppermute | solution.py:15
  76.1 62.7 %collective-permute-start.8 = (bf16[2,128]{1,0:T(2,128)(2,1)S(1)}, bf16[2,128]{1,0:T(2,128)(2,1)S(1)}, u32[]{:S(2)}, u32[]{:S(2)}) collective-permute-start(bf16[2,128]{1,0:T(2,128)(2,1)S(1)} %convert_element_type.241), channel_id=1, source_target_pairs={{0,12},{4,16},{8,20},{12,24},{16,28},{20,32},{24,36},{28,40},{32,4... | collective-permute-start | bytes 1544 | tf_op jit(solution)/shard_map/ppermute | solution.py:15
  98.3 42.3 %collective-permute-start.12 = (bf16[2,128]{1,0:T(2,128)(2,1)S(1)}, bf16[2,128]{1,0:T(2,128)(2,1)S(1)}, u32[]{:S(2)}, u32[]{:S(2)}) collective-permute-start(bf16[2,128]{1,0:T(2,128)(2,1)S(1)} %convert_element_type.245), channel_id=1, source_target_pairs={{0,16},{4,20},{8,24},{12,28},{16,32},{20,36},{24,40},{28,44},{32,4... | collective-permute-start | bytes 1544 | tf_op jit(solution)/shard_map/ppermute | solution.py:15
  100.4 40.3 %collective-permute-start.16 = (bf16[2,128]{1,0:T(2,128)(2,1)S(1)}, bf16[2,128]{1,0:T(2,128)(2,1)S(1)}, u32[]{:S(2)}, u32[]{:S(2)}) collective-permute-start(bf16[2,128]{1,0:T(2,128)(2,1)S(1)} %convert_element_type.249), channel_id=1, source_target_pairs={{0,20},{4,24},{8,28},{12,32},{16,36},{20,40},{24,44},{28,48},{32,5... | collective-permute-start | bytes 1544 | tf_op jit(solution)/shard_map/ppermute | solution.py:15
  154.7 22.1 %collective-permute-start.13 = (bf16[2,64,4,64]{3,1,2,0:T(8,128)(2,1)}, bf16[2,64,4,64]{3,1,2,0:T(8,128)(2,1)}, u32[]{:S(2)}, u32[]{:S(2)}) collective-permute-start(bf16[2,64,4,64]{3,1,2,0:T(8,128)(2,1)} %gather_fusion.2), channel_id=1, source_target_pairs={{0,16},{4,20},{8,24},{12,28},{16,32},{20,36},{24,40},{28,44},{32,4... | collective-permute-start | bytes 196616 | tf_op jit(solution)/shard_map/ppermute | solution.py:15
  156.9 25.3 %collective-permute-start.17 = (bf16[2,64,4,64]{3,1,2,0:T(8,128)(2,1)}, bf16[2,64,4,64]{3,1,2,0:T(8,128)(2,1)}, u32[]{:S(2)}, u32[]{:S(2)}) collective-permute-start(bf16[2,64,4,64]{3,1,2,0:T(8,128)(2,1)} %gather_fusion.2), channel_id=1, source_target_pairs={{0,20},{4,24},{8,28},{12,32},{16,36},{20,40},{24,44},{28,48},{32,5... | collective-permute-start | bytes 196616 | tf_op jit(solution)/shard_map/ppermute | solution.py:15
  158.4 29.3 %collective-permute-start.21 = (bf16[2,64,4,64]{3,1,2,0:T(8,128)(2,1)}, bf16[2,64,4,64]{3,1,2,0:T(8,128)(2,1)}, u32[]{:S(2)}, u32[]{:S(2)}) collective-permute-start(bf16[2,64,4,64]{3,1,2,0:T(8,128)(2,1)} %gather_fusion.2), channel_id=1, source_target_pairs={{0,24},{4,28},{8,32},{12,36},{16,40},{20,44},{24,48},{28,52},{32,5... | collective-permute-start | bytes 196616 | tf_op jit(solution)/shard_map/ppermute | solution.py:15
  170.9 18.4 %collective-permute-start.25 = (bf16[2,64,4,64]{3,1,2,0:T(8,128)(2,1)S(1)}, bf16[2,64,4,64]{3,1,2,0:T(8,128)(2,1)S(1)}, u32[]{:S(2)}, u32[]{:S(2)}) collective-permute-start(bf16[2,64,4,64]{3,1,2,0:T(8,128)(2,1)S(1)} %copy-done.31), channel_id=1, source_target_pairs={{0,28},{4,32},{8,36},{12,40},{16,44},{20,48},{24,52},{28,56},{32,6... | collective-permute-start | bytes 196616 | tf_op jit(solution)/shard_map/ppermute | solution.py:15
  172.9 20.0 %collective-permute-start.35 = (f32[2,4,64]{2,1,0:T(4,128)S(1)}, f32[2,4,64]{2,1,0:T(4,128)S(1)}, u32[]{:S(2)}, u32[]{:S(2)}) collective-permute-start(f32[2,4,64]{2,1,0:T(4,128)S(1)} %convert_reduce_fusion.8), channel_id=1, source_target_pairs={{0,248},{4,252},{8,0},{12,4},{16,8},{20,12},{24,16},{28,20},{32,24... | collective-permute-start | bytes 6152 | tf_op jit(solution)/shard_map/ppermute | solution.py:15
  204.2 56.2 %collective-permute-start.1 = (bf16[8,64,4,64]{3,1,2,0:T(8,128)(2,1)}, bf16[8,64,4,64]{3,1,2,0:T(8,128)(2,1)}, u32[]{:S(2)}, u32[]{:S(2)}) collective-permute-start(bf16[8,64,4,64]{3,1,2,0:T(8,128)(2,1)} %copy.159), channel_id=1, source_target_pairs={{0,4},{4,8},{8,12},{12,16},{16,20},{20,24},{24,28},{28,32},{32,36}... | collective-permute-start | bytes 786440 | tf_op jit(solution)/shard_map/ppermute | solution.py:15
  210.9 30.3 %collective-permute-start.14 = (f32[2,64,4,64]{1,3,2,0:T(8,128)}, f32[2,64,4,64]{1,3,2,0:T(8,128)}, u32[]{:S(2)}, u32[]{:S(2)}) collective-permute-start(f32[2,64,4,64]{1,3,2,0:T(8,128)} %convolution_bitcast_fusion.6), channel_id=1, source_target_pairs={{0,240},{4,244},{8,248},{12,252},{16,0},{20,4},{24,8},{28,12},{32,... | collective-permute-start | bytes 393224 | tf_op jit(solution)/shard_map/ppermute | solution.py:15
  213.1 32.8 %collective-permute-start.18 = (f32[2,64,4,64]{1,3,2,0:T(8,128)}, f32[2,64,4,64]{1,3,2,0:T(8,128)}, u32[]{:S(2)}, u32[]{:S(2)}) collective-permute-start(f32[2,64,4,64]{1,3,2,0:T(8,128)} %convolution_bitcast_fusion.5), channel_id=1, source_target_pairs={{0,236},{4,240},{8,244},{12,248},{16,252},{20,0},{24,4},{28,8},{32... | collective-permute-start | bytes 393224 | tf_op jit(solution)/shard_map/ppermute | solution.py:15
  218.3 32.5 %collective-permute-start.22 = (f32[2,64,4,64]{1,3,2,0:T(8,128)}, f32[2,64,4,64]{1,3,2,0:T(8,128)}, u32[]{:S(2)}, u32[]{:S(2)}) collective-permute-start(f32[2,64,4,64]{1,3,2,0:T(8,128)} %convolution_bitcast_fusion.4), channel_id=1, source_target_pairs={{0,232},{4,236},{8,240},{12,244},{16,248},{20,252},{24,0},{28,4},{... | collective-permute-start | bytes 393224 | tf_op jit(solution)/shard_map/ppermute | solution.py:15
  223.8 31.8 %collective-permute-start.26 = (f32[2,64,4,64]{1,3,2,0:T(8,128)}, f32[2,64,4,64]{1,3,2,0:T(8,128)}, u32[]{:S(2)}, u32[]{:S(2)}) collective-permute-start(f32[2,64,4,64]{1,3,2,0:T(8,128)} %convolution_bitcast_fusion.3), channel_id=1, source_target_pairs={{0,228},{4,232},{8,236},{12,240},{16,244},{20,248},{24,252},{28,0}... | collective-permute-start | bytes 393224 | tf_op jit(solution)/shard_map/ppermute | solution.py:15
  300.6 105.7 %reduce-scatter.2.cloned.1.call-start = ((), (), s32[]{:S(2)}) async-start(), calls=%async_computation.3 | async-start | bytes 1310720 | tf_op jit(solution)/shard_map/reduce_scatter | solution.py:170
  (68 other events, 1112.5 us)
Sparse Core Ops, SparseCore 0:
  17.5 30.9 all-gather.1
  300.7 66.6 all-reduce.2
  380.4 25.8 reduce-scatter.1
where the time goes:
time: 430 us; the launch traced here: 425 us
  waiting for transfers between devices  105 us (24%)
  local copies, waits for them, and re-layouts  102 us (24%)
  matrix products  102 us (24%)
  starting transfers between devices  72.5 us (17%)
  other arithmetic  19.6 us (5%)
  between operations  15.3 us (4%)
  blocking collectives  8.47 us (2%)
    ppermute x41, starting transfers between devices, from_behind(): lax.ppermute(value, axis, [(i, (i + by) % size) for i in range(size)])  72.2 us
    psum x1, waiting for transfers between devices, shards(): summed = lax.psum(branch, 'tp')  66.8 us
    dot_general x8, matrix products, page_rows(): jnp.einsum('rs,spcf->rpcf', picker, cache_pool, preferred_element_type=jn...  64.3 us
    reduce_scatter x1, waiting for transfers between devices, shards(): lax.psum_scatter(jnp.dot(inner, w_down, preferred_element_type=jnp.float3...  22.1 us
    slice x16, local copies, waits for them, and re-layouts, rows_split(): rows[:, :, 0].reshape(requests, page_len, heads_local, HD)  19.2 us
    scatter x12, local copies, waits for them, and re-layouts, spread_back(): jnp.zeros((requests,) + arrived[0].shape[1:], jnp.float32).at[long_ids]  17.2 us
    ppermute x41, waiting for transfers between devices, from_behind(): lax.ppermute(value, axis, [(i, (i + by) % size) for i in range(size)])  16.4 us
    unnamed x119, local copies, waits for them, and re-layouts  14.9 us
  transfers between devices with their start and end apart: 44, of which 6 were waited for; matrix products, arithmetic and copies ran while one was open for 42% of the time, Pallas kernels for 0%

commit v1 on v0

v1 whole, which is shorter than its diff:
```python
import functools

import jax
import jax.numpy as jnp
from jax import lax
from jax.experimental import pallas as pl
from jax.experimental.pallas import tpu as pltpu
from jax.sharding import PartitionSpec as P

HD = 64
NEG = -1e30
EPS = 1e-05
BF = jnp.bfloat16
F32 = jnp.float32
MESH = pl.DeviceIdType.MESH
VMEM_BYTES = 60 * 2**20


def dot(a, b):
    return jnp.dot(a, b, preferred_element_type=F32)


def dot_t(a, b):
    return lax.dot_general(a, b, (((1,), (1,)), ((), ())), preferred_element_type=F32)


def iota(shape, dim):
    return lax.broadcasted_iota(jnp.int32, shape, dim)


def remote(src, dst, ssem, rsem, dev):
    return pltpu.make_async_remote_copy(
        src_ref=src, dst_ref=dst, send_sem=ssem, recv_sem=rsem, device_id=dev, device_id_type=MESH
    )


def greet(devices):
    barrier = pltpu.get_barrier_semaphore()
    for dev in devices:
        pl.semaphore_signal(barrier, inc=1, device_id=dev, device_id_type=MESH)
    pl.semaphore_wait(barrier, len(devices))


def project_kernel(
    sizes,
    hidden,
    weights,
    parents,
    accept,
    lens_row,
    x_out,
    q_out,
    k_out,
    v_out,
    reach_out,
    select_out,
    lens_out,
    xbuf,
    lbuf,
    xs,
    xr,
    ls,
    lr,
):
    n_req, n_tp, pages, chunks = sizes
    e = lax.axis_index("req")
    t = lax.axis_index("tp")
    rows = hidden.shape[0] // chunks
    share = hidden.shape[1]
    peers = [(e, lax.rem(t + r, n_tp)) for r in range(1, n_tp)]
    after = [(lax.rem(e + j, n_req), t) for j in range(1, pages)]
    before = [(lax.rem(e - j + n_req, n_req), t) for j in range(1, pages)]
    greet(peers + after + before)

    def len_copy(j):
        return remote(lens_row, lbuf.at[j - 1], ls.at[j - 1], lr.at[j - 1], after[j - 1])

    def x_copy(r, c):
        span = pl.ds(c * rows, rows)
        return remote(
            hidden.at[span], xbuf.at[r - 1, span], xs.at[r - 1, c], xr.at[r - 1, c], peers[r - 1]
        )

    for j in range(1, pages):
        len_copy(j).start()
    order = [1, 3, 2] if n_tp == 4 else list(range(1, n_tp))
    for c in range(chunks):
        for r in order:
            x_copy(r, c).start()

    requests, draft = parents.shape
    per = 256 // draft
    wide = per * draft
    for g in range(requests // per):
        line = jnp.concatenate(
            [
                jnp.where(parents[g * per + b : g * per + b + 1, :] < 0, -1, parents[g * per + b : g * per + b + 1, :] + b * draft)
                for b in range(per)
            ],
            axis=1,
        )
        low = iota((wide, wide), 0)
        high = iota((wide, wide), 1)
        up = jnp.where((low == line) | (low == high), 1.0, 0.0)
        steps = max(1, (draft - 1).bit_length())
        for _ in range(steps - 1):
            up = jnp.minimum(dot(up.astype(BF), up.astype(BF)), 1.0)
        last = up.astype(BF)
        up = jnp.minimum(dot(last, last), 1.0)
        down = jnp.swapaxes(up, 0, 1)
        depth = jnp.sum(up, axis=0, keepdims=True) - 1.0
        hit = low == -1
        for b in range(per):
            hit = hit | (low == accept[g * per + b] + b * draft)
        chosen = jnp.sum(jnp.where(hit, down, 0.0), axis=0, keepdims=True)
        level = iota((draft, wide), 0).astype(F32)
        select = jnp.where(level == depth, chosen, 0.0)
        select_out[g] = select.astype(BF)
        for b in range(per):
            span = slice(b * draft, (b + 1) * draft)
            reach_out[g * per + b] = down[span, span]

    for c in range(chunks):
        span = pl.ds(c * rows, rows)
        x_out[span, pl.ds(pl.multiple_of(t * share, share), share)] = hidden[span]
        for r in range(1, n_tp):
            x_copy(r, c).wait_recv()
            s = lax.rem(t - r + n_tp, n_tp)
            x_out[span, pl.ds(pl.multiple_of(s * share, share), share)] = xbuf[r - 1, span]
        x = x_out[span]
        both = (dot(x, weights[0]) * 0.125).astype(BF)
        for i in range(rows // draft):
            q_out[c * rows // draft + i] = both[i * draft : (i + 1) * draft]
        k_out[span] = dot(x, weights[1]).astype(BF)
        v_out[span] = dot(x, weights[2]).astype(BF)

    for j in range(1, pages):
        len_copy(j).wait_recv()
    lens_out[...] = lbuf[...]
    for j in range(1, pages):
        len_copy(j).wait_send()
    for c in range(chunks):
        for r in range(1, n_tp):
            x_copy(r, c).wait_send()


def project(sizes, hidden, weights, parents, accept, lens_row):
    n_req, n_tp, pages, chunks = sizes
    tokens, share = hidden.shape
    requests, draft = parents.shape
    width = weights.shape[2]
    vm = pl.BlockSpec(memory_space=pltpu.VMEM)
    sm = pl.BlockSpec(memory_space=pltpu.SMEM)
    sds = jax.ShapeDtypeStruct
    return pl.pallas_call(
        functools.partial(project_kernel, sizes),
        out_shape=(
            sds((tokens, share * n_tp), BF),
            sds((requests, draft, width), BF),
            sds((tokens, width), BF),
            sds((tokens, width), BF),
            sds((requests, draft, draft), F32),
            sds((requests * draft // 256, draft, 256), BF),
            sds((pages - 1, 1, 128), jnp.int32),
        ),
        in_specs=[vm, vm, vm, sm, vm],
        out_specs=(vm,) * 7,
        scratch_shapes=[
            pltpu.VMEM((n_tp - 1, tokens, share), BF),
            pltpu.VMEM((pages - 1, 1, 128), jnp.int32),
            pltpu.SemaphoreType.DMA((n_tp - 1, chunks)),
            pltpu.SemaphoreType.DMA((n_tp - 1, chunks)),
            pltpu.SemaphoreType.DMA((pages - 1,)),
            pltpu.SemaphoreType.DMA((pages - 1,)),
        ],
        compiler_params=pltpu.CompilerParams(
            collective_id=0, has_side_effects=True, vmem_limit_bytes=VMEM_BYTES
        ),
        name="gather_project",
    )(hidden, weights, parents, accept, lens_row)


def diagonal(rows64, mask):
    return jnp.concatenate([rows64] * 4, axis=0) * mask


def fold(wide, draft):
    lane = iota((draft, wide.shape[1]), 1)
    out = wide[0:draft]
    for h in range(1, wide.shape[1] // HD):
        out = jnp.where(lane >= h * HD, wide[h * draft : (h + 1) * draft], out)
    return out


def page_part(queries, page, count, draft):
    scores = pltpu.roll(dot_t(queries, page), 1, 1)
    lane = iota(scores.shape, 1)
    valid = (lane < 2 * count) & (lax.rem(lane, 2) == 1)
    top = jnp.max(jnp.where(valid, scores, NEG), axis=1, keepdims=True)
    weights = jnp.where(valid, jnp.exp(scores - top), 0.0).astype(BF)
    total = jnp.sum(weights.astype(F32), axis=1, keepdims=True)
    return fold(dot(weights, page), draft), top, total


def spread(column, draft):
    lane = iota((draft, 128), 1)
    tiles = []
    for i in range(2):
        a = jnp.broadcast_to(column[2 * i * draft : (2 * i + 1) * draft], (draft, 128))
        b = jnp.broadcast_to(column[(2 * i + 1) * draft : (2 * i + 2) * draft], (draft, 128))
        tiles.append(jnp.where(lane < HD, a, b))
    return jnp.concatenate(tiles, axis=1)


def place(stats, column, at):
    lane = iota(stats.shape, 1)
    return jnp.where(lane == at, column, stats)


def attend_kernel(
    sizes,
    q,
    k,
    v,
    reach,
    select,
    w_own,
    page_table,
    own_len,
    far_len,
    pool,
    att_out,
    kept_k,
    kept_v,
    w_out,
    pages_v,
    qlong,
    q_one,
    q_far,
    part_one,
    stat_one,
    part_far,
    stat_far,
    back_one,
    bstat_one,
    back_far,
    bstat_far,
    acc,
    own_stat,
    wbuf,
    psem,
    q1s,
    q1r,
    qfs,
    qfr,
    p1s,
    p1r,
    t1s,
    t1r,
    pfs,
    pfr,
    tfs,
    tfr,
    ws,
    wr,
    fs,
    fr,
):
    n_req, n_tp, pages, _ = sizes
    e = lax.axis_index("req")
    t = lax.axis_index("tp")
    requests, draft, _ = reach.shape
    page_len = pages_v.shape[1]
    longs = (requests + 3) // 4
    half = w_own.shape[0] // 2
    parity = lax.rem(e, 2)
    partner = (e + 1 - 2 * parity, t)
    peers = [(e, lax.rem(t + r, n_tp)) for r in range(1, n_tp)]

    def ahead(j):
        return (lax.rem(e + j, n_req), t)

    def behind(j):
        return (lax.rem(e - j + n_req, n_req), t)

    load = pltpu.make_async_copy(pool, pages_v, psem)
    load.start()

    def long_pair(length):
        first = jnp.int32(requests)
        second = jnp.int32(0)
        for m in range(requests):
            is_long = length(m) > 2 * page_len
            first = jnp.where(is_long, jnp.minimum(first, m), first)
            second = jnp.where(is_long, jnp.maximum(second, m), second)
        return jnp.minimum(first, requests - 1), second

    mine = long_pair(lambda m: own_len[m])
    for i in range(longs):
        qlong[i] = q[mine[i]]

    greet(peers + [ahead(j) for j in range(1, pages)] + [behind(j) for j in range(1, pages)])

    quarters = requests // 2

    def far_q(j):
        return remote(qlong, q_far.at[j - 2], qfs.at[j - 2], qfr.at[j - 2], ahead(j))

    def one_q(c):
        span = pl.ds(2 * c, 2)
        return remote(q.at[span], q_one.at[span], q1s.at[c], q1r.at[c], ahead(1))

    def one_part(c):
        return remote(part_one.at[c], back_one.at[c], p1s.at[c], p1r.at[c], behind(1))

    def one_stat():
        return remote(stat_one, bstat_one, t1s, t1r, behind(1))

    def far_part(j):
        return remote(part_far.at[j - 2], back_far.at[j - 2], pfs.at[j - 2], pfr.at[j - 2], behind(j))

    def far_stat(j):
        return remote(stat_far.at[j - 2], bstat_far.at[j - 2], tfs.at[j - 2], tfr.at[j - 2], behind(j))

    def w_copy(r):
        return remote(
            w_own.at[pl.ds(pl.multiple_of(parity * half, half), half)],
            wbuf.at[r - 1, parity],
            ws.at[r - 1],
            wr.at[r - 1],
            peers[r - 1],
        )

    def w_pass(r):
        return remote(wbuf.at[r - 1, parity], wbuf.at[r - 1, parity], fs.at[r - 1], fr.at[r - 1], partner)

    for j in range(pages - 1, 1, -1):
        far_q(j).start()
    for c in range(quarters):
        one_q(c).start()
    for r in range(1, n_tp):
        w_copy(r).start()

    width = q.shape[2]
    mask = jnp.where(
        iota((4 * draft, width), 0) // draft == iota((4 * draft, width), 1) // HD, 1.0, 0.0
    ).astype(BF)

    load.wait()

    def page_of(slot):
        return pages_v[slot].reshape(2 * page_len, width)

    for r in range(requests):
        rows = slice(r * draft, (r + 1) * draft)
        queries = diagonal(q[r], mask)
        part, top, total = page_part(queries, page_of(page_table[0, r]), own_len[r], draft)
        allowed = jnp.concatenate([reach[r]] * 4, axis=0) > 0.5
        scores = dot_t(queries, k[rows])
        tree_top = jnp.max(jnp.where(allowed, scores, NEG), axis=1, keepdims=True)
        best = jnp.maximum(top, tree_top)
        weights = jnp.where(allowed, jnp.exp(scores - best), 0.0).astype(BF)
        scale = jnp.exp(top - best)
        total = total * scale + jnp.sum(weights.astype(F32), axis=1, keepdims=True)
        tree = fold(dot(weights, v[rows]), draft)
        acc[r] = part * spread(scale, draft) + tree
        own_stat[r] = place(place(jnp.zeros((4 * draft, 128), F32), best, 0), total, 1)

    for j in range(pages - 1, 1, -1):
        pair = long_pair(lambda m: far_len[j - 1, 0, m])
        far_q(j).wait_recv()
        stats = jnp.zeros((4 * draft, 128), F32)
        for i in range(longs):
            slot = page_table[j, 0]
            count = far_len[j - 1, 0, 0]
            for m in range(1, requests):
                slot = jnp.where(pair[i] == m, page_table[j, m], slot)
                count = jnp.where(pair[i] == m, far_len[j - 1, 0, m], count)
            count = count - j * page_len
            queries = diagonal(q_far[j - 2, i], mask)
            part, top, total = page_part(queries, page_of(slot), count, draft)
            part_far[j - 2, i * draft : (i + 1) * draft] = part.astype(BF)
            stats = place(place(stats, top, 2 * i), total, 2 * i + 1)
        stat_far[j - 2] = jnp.swapaxes(stats, 0, 1)[0:8]
        far_part(j).start()
        far_stat(j).start()

    stats = jnp.zeros((4 * draft, 128), F32)
    for c in range(quarters):
        one_q(c).wait_recv()
        for i in range(2):
            r = 2 * c + i
            count = far_len[0, 0, r] - page_len
            queries = diagonal(q_one[r], mask)
            part, top, total = page_part(queries, page_of(page_table[1, r]), count, draft)
            part_one[c, i * draft : (i + 1) * draft] = part.astype(BF)
            stats = place(place(stats, top, 2 * r), total, 2 * r + 1)
        one_part(c).start()
    stat_one[...] = jnp.swapaxes(stats, 0, 1)[0:16]
    one_stat().start()

    for r in range(1, n_tp):
        w_copy(r).wait_recv()
        w_pass(r).start()

    per = 256 // draft
    for r in range(requests):
        rows = slice(r * draft, (r + 1) * draft)
        b = r % per
        pick = select[r // per][:, b * draft : (b + 1) * draft]
        kept_k[r] = dot(pick, k[rows]).astype(BF)
        kept_v[r] = dot(pick, v[rows]).astype(BF)

    for j in range(pages - 1, 1, -1):
        far_stat(j).wait_recv()
    far_columns = jnp.swapaxes(
        jnp.concatenate(
            [bstat_far[j - 2] for j in range(2, pages)]
            + [jnp.zeros((128 - 8 * (pages - 2), 4 * draft), F32)],
            axis=0,
        ),
        0,
        1,
    )
    for j in range(pages - 1, 1, -1):
        far_part(j).wait_recv()
    long_acc = []
    long_top = []
    long_total = []
    for i in range(longs):
        tops = [far_columns[:, 8 * (j - 2) + 2 * i : 8 * (j - 2) + 2 * i + 1] for j in range(2, pages)]
        sums = [far_columns[:, 8 * (j - 2) + 2 * i + 1 : 8 * (j - 2) + 2 * i + 2] for j in range(2, pages)]
        best = functools.reduce(jnp.maximum, tops)
        total = jnp.zeros_like(best)
        out = jnp.zeros((draft, width), F32)
        for j in range(2, pages):
            scale = jnp.exp(tops[j - 2] - best)
            total = total + scale * sums[j - 2]
            out = out + spread(scale, draft) * back_far[j - 2, i * draft : (i + 1) * draft].astype(F32)
        long_acc.append(out)
        long_top.append(best)
        long_total.append(total)

    one_stat().wait_recv()
    one_columns = jnp.swapaxes(
        jnp.concatenate([bstat_one[...], jnp.zeros((128 - 16, 4 * draft), F32)], axis=0), 0, 1
    )
    for c in range(quarters):
        one_part(c).wait_recv()
        for i in range(2):
            r = 2 * c + i
            tall = (4 * draft, 1)
            second = jnp.full(tall, mine[1], jnp.int32) == r
            is_long = jnp.full(tall, own_len[r], jnp.int32) > 2 * page_len
            top_l = jnp.where(is_long, jnp.where(second, long_top[1], long_top[0]), NEG)
            total_l = jnp.where(second, long_total[1], long_total[0])
            acc_l = jnp.where(
                jnp.full((draft, width), mine[1], jnp.int32) == r, long_acc[1], long_acc[0]
            )
            stat = own_stat[r]
            top_o = stat[:, 0:1]
            total_o = stat[:, 1:2]
            top_1 = one_columns[:, 2 * r : 2 * r + 1]
            total_1 = one_columns[:, 2 * r + 1 : 2 * r + 2]
            best = jnp.maximum(jnp.maximum(top_o, top_1), top_l)
            s_o = jnp.exp(top_o - best)
            s_1 = jnp.exp(top_1 - best)
            s_l = jnp.exp(top_l - best)
            whole = 1.0 / (s_o * total_o + s_1 * total_1 + s_l * total_l)
            out = acc[r] * spread(s_o * whole, draft)
            out = out + back_one[c, i * draft : (i + 1) * draft].astype(F32) * spread(s_1 * whole, draft)
            out = out + acc_l * spread(s_l * whole, draft)
            att_out[r * draft : (r + 1) * draft] = out.astype(BF)

    for r in range(1, n_tp):
        remote(
            wbuf.at[r - 1, 1 - parity], wbuf.at[r - 1, 1 - parity], fs.at[r - 1], fr.at[r - 1], partner
        ).wait_recv()
        for h in range(2):
            w_out[r - 1, h * half : (h + 1) * half] = wbuf[r - 1, h]

    for j in range(2, pages):
        far_q(j).wait_send()
        far_part(j).wait_send()
        far_stat(j).wait_send()
    for c in range(quarters):
        one_q(c).wait_send()
        one_part(c).wait_send()
    one_stat().wait_send()
    for r in range(1, n_tp):
        w_copy(r).wait_send()
        w_pass(r).wait_send()


def attend(sizes, q, k, v, reach, select, w_own, page_table, own_len, far_len, pool):
    n_req, n_tp, pages, _ = sizes
    requests, draft, width = q.shape
    tokens = requests * draft
    slots, page_len = pool.shape[0], pool.shape[1]
    rows_w, cols_w = w_own.shape
    quarters = requests // 2
    far = pages - 2
    vm = pl.BlockSpec(memory_space=pltpu.VMEM)
    sm = pl.BlockSpec(memory_space=pltpu.SMEM)
    sds = jax.ShapeDtypeStruct
    dma = pltpu.SemaphoreType.DMA
    return pl.pallas_call(
        functools.partial(attend_kernel, sizes),
        out_shape=(
            sds((tokens, width), BF),
            sds((requests, draft, width), BF),
            sds((requests, draft, width), BF),
            sds((n_tp - 1, rows_w, cols_w), BF),
        ),
        in_specs=[vm, vm, vm, vm, vm, vm, sm, sm, sm, pl.BlockSpec(memory_space=pl.ANY)],
        out_specs=(vm,) * 4,
        scratch_shapes=[
            pltpu.VMEM((slots, page_len, 2, width), BF),
            pltpu.VMEM((2, draft, width), BF),
            pltpu.VMEM((requests, draft, width), BF),
            pltpu.VMEM((far, 2, draft, width), BF),
            pltpu.VMEM((quarters, 2 * draft, width), BF),
            pltpu.VMEM((16, 4 * draft), F32),
            pltpu.VMEM((far, 2 * draft, width), BF),
            pltpu.VMEM((far, 8, 4 * draft), F32),
            pltpu.VMEM((quarters, 2 * draft, width), BF),
            pltpu.VMEM((16, 4 * draft), F32),
            pltpu.VMEM((far, 2 * draft, width), BF),
            pltpu.VMEM((far, 8, 4 * draft), F32),
            pltpu.VMEM((requests, draft, width), F32),
            pltpu.VMEM((requests, 4 * draft, 128), F32),
            pltpu.VMEM((n_tp - 1, 2, rows_w // 2, cols_w), BF),
            dma,
            dma((quarters,)),
            dma((quarters,)),
            dma((far,)),
            dma((far,)),
            dma((quarters,)),
            dma((quarters,)),
            dma,
            dma,
            dma((far,)),
            dma((far,)),
            dma((far,)),
            dma((far,)),
            dma((n_tp - 1,)),
            dma((n_tp - 1,)),
            dma((n_tp - 1,)),
            dma((n_tp - 1,)),
        ],
        compiler_params=pltpu.CompilerParams(
            collective_id=1, has_side_effects=True, vmem_limit_bytes=VMEM_BYTES
        ),
        name="attend",
    )(q, k, v, reach, select, w_own, page_table, own_len, far_len, pool)


def finish_kernel(
    sizes,
    att,
    x,
    w_own,
    w_far,
    w_up,
    w_down,
    gain1,
    gain2,
    out,
    abuf,
    normed_v,
    share_v,
    obuf,
    rbuf,
    second,
    srow,
    sbuf,
    as_,
    ar,
    os_,
    or_,
    ss,
    sr,
):
    n_req, n_tp, pages, chunks = sizes
    e = lax.axis_index("req")
    t = lax.axis_index("tp")
    tokens, share = att.shape
    rows = tokens // chunks
    width = x.shape[1]
    peers = [(e, lax.rem(t + r, n_tp)) for r in range(1, n_tp)]
    greet(peers)

    def a_copy(r, c):
        span = pl.ds(c * rows, rows)
        return remote(
            att.at[span], abuf.at[r - 1, span], as_.at[r - 1, c], ar.at[r - 1, c], peers[r - 1]
        )

    def o_copy(r, c):
        s = lax.rem(t + r, n_tp)
        span = pl.ds(c * rows, rows)
        return remote(
            obuf.at[span, pl.ds(pl.multiple_of(s * share, share), share)],
            rbuf.at[r - 1, span],
            os_.at[r - 1, c],
            or_.at[r - 1, c],
            peers[r - 1],
        )

    def s_copy(r):
        return remote(srow, sbuf.at[r - 1], ss.at[r - 1], sr.at[r - 1], peers[r - 1])

    order = [1, 3, 2] if n_tp == 4 else list(range(1, n_tp))
    for c in range(chunks):
        for r in order:
            a_copy(r, c).start()

    mine = pl.ds(pl.multiple_of(t * share, share), share)
    for c in range(chunks):
        span = pl.ds(c * rows, rows)
        branch = dot(att[span], w_own[...])
        for r in range(1, n_tp):
            a_copy(r, c).wait_recv()
            branch = branch + dot(abuf[r - 1, span], w_far[r - 1])
        z = x[span].astype(F32) + branch
        center = jnp.sum(z, axis=1, keepdims=True) / width
        var = jnp.sum(z * z, axis=1, keepdims=True) / width - center * center
        normed = ((z - center) * lax.rsqrt(var + EPS) * gain1[...]).astype(BF)
        normed_v[...] = normed
        share_v[span] = normed_v[:, mine]
        pre = dot(normed, w_up[...])
        inner = (0.5 * pre * (1.0 + lax.erf(pre * 0.7071067811865476))).astype(BF)
        obuf[span] = dot(inner, w_down[...]).astype(BF)
        for r in order:
            o_copy(r, c).start()

    lane = iota((rows, 128), 1)
    stats = jnp.zeros((rows, 128), F32)
    for c in range(chunks):
        span = pl.ds(c * rows, rows)
        y = share_v[span].astype(F32) + obuf[span, mine].astype(F32)
        for r in range(1, n_tp):
            o_copy(r, c).wait_recv()
            y = y + rbuf[r - 1, span].astype(F32)
        second[span] = y
        stats = jnp.where(lane == 2 * c, jnp.sum(y, axis=1, keepdims=True), stats)
        stats = jnp.where(lane == 2 * c + 1, jnp.sum(y * y, axis=1, keepdims=True), stats)
    total = jnp.swapaxes(stats, 0, 1)[0:8]
    srow[...] = total
    for r in order:
        s_copy(r).start()
    for r in range(1, n_tp):
        s_copy(r).wait_recv()
        total = total + sbuf[r - 1]
    columns = jnp.swapaxes(
        jnp.concatenate([total, jnp.zeros((128 - 8, rows), F32)], axis=0), 0, 1
    )
    for c in range(chunks):
        span = pl.ds(c * rows, rows)
        center = columns[:, 2 * c : 2 * c + 1] / width
        var = columns[:, 2 * c + 1 : 2 * c + 2] / width - center * center
        out[span] = ((second[span] - center) * lax.rsqrt(var + EPS) * gain2[:, mine]).astype(BF)

    for r in range(1, n_tp):
        s_copy(r).wait_send()
        for c in range(chunks):
            a_copy(r, c).wait_send()
            o_copy(r, c).wait_send()


def finish(sizes, att, x, w_own, w_far, w_up, w_down, gain1, gain2):
    n_req, n_tp, pages, chunks = sizes
    tokens, share = att.shape
    width = x.shape[1]
    rows = tokens // chunks
    vm = pl.BlockSpec(memory_space=pltpu.VMEM)
    dma = pltpu.SemaphoreType.DMA
    return pl.pallas_call(
        functools.partial(finish_kernel, sizes),
        out_shape=jax.ShapeDtypeStruct((tokens, share), BF),
        in_specs=[vm] * 8,
        out_specs=vm,
        scratch_shapes=[
            pltpu.VMEM((n_tp - 1, tokens, share), BF),
            pltpu.VMEM((rows, width), BF),
            pltpu.VMEM((tokens, share), BF),
            pltpu.VMEM((tokens, width), BF),
            pltpu.VMEM((n_tp - 1, tokens, share), BF),
            pltpu.VMEM((tokens, share), F32),
            pltpu.VMEM((8, rows), F32),
            pltpu.VMEM((n_tp - 1, 8, rows), F32),
            dma((n_tp - 1, chunks)),
            dma((n_tp - 1, chunks)),
            dma((n_tp - 1, chunks)),
            dma((n_tp - 1, chunks)),
            dma((n_tp - 1,)),
            dma((n_tp - 1,)),
        ],
        compiler_params=pltpu.CompilerParams(
            collective_id=2, has_side_effects=True, vmem_limit_bytes=VMEM_BYTES
        ),
        name="finish",
    )(att, x, w_own, w_far, w_up, w_down, gain1.reshape(1, -1), gain2.reshape(1, -1))


def shards(
    sizes,
    hidden_in,
    w_qkv,
    w_out,
    first_gain,
    w_up,
    w_down,
    second_gain,
    cache_pool,
    page_table,
    cache_len,
    tree_parent,
    accept_node,
):
    requests = tree_parent.shape[0]
    lens_row = jnp.pad(cache_len, (0, 128 - requests)).reshape(1, 128)
    x, q, k, v, reach, select, far_len = project(
        sizes, hidden_in, jnp.transpose(w_qkv, (1, 0, 2)), tree_parent, accept_node, lens_row
    )
    att, kept_k, kept_v, w_far = attend(
        sizes, q, k, v, reach, select, w_out, page_table, cache_len, far_len, cache_pool
    )
    layer_out = finish(sizes, att, x, w_out, w_far, w_up, w_down, first_gain, second_gain)
    return layer_out, jnp.stack([kept_k, kept_v], axis=2)


def solution(mesh):
    placed = (
        P("req", "tp"),
        P(None, None, "tp"),
        P("tp", None),
        P(),
        P(None, "tp"),
        P("tp", None),
        P(),
        P("req", None, None, "tp"),
        P("req", None),
        P("req"),
        P("req", None),
        P("req"),
    )
    sizes = (mesh.shape["req"], mesh.shape["tp"], 8, 4)
    return jax.shard_map(
        functools.partial(shards, sizes),
        mesh=mesh,
        in_specs=placed,
        out_specs=(P("req", "tp"), P("req", None, None, "tp")),
        check_vma=False,
    )
```

time: 430 us -> 101 us (0.23)
  the two profiles are of different devices: /device:TPU:2 before, /device:TPU:1 now
where the time goes in v1:
time: 101 us
  Pallas kernels  97.1 us (96%)
  local copies, waits for them, and re-layouts  3.22 us (3%)
    pallas_call x1, Pallas kernels, attend(): pl.pallas_call(functools.partial(attend_kernel, sizes), out_shape=(sds((t...  35 us
    pallas_call x1, Pallas kernels, finish(): pl.pallas_call(functools.partial(finish_kernel, sizes), out_shape=jax.Sha...  34 us
    pallas_call x1, Pallas kernels, project(): pl.pallas_call(functools.partial(project_kernel, sizes), out_shape=(sds((...  28.1 us
    unnamed x8, local copies, waits for them, and re-layouts  2.05 us

profile of v1, /device:TPU:1, one launch (start us, length us, event | category | flops | bytes accessed | tf_op | source)
XLA Modules:
  0.0 101.1 jit_solution(6474959407433958880)
XLA Ops:
  0.6 1.2 %pad_bitcast_fusion.lens_row = s32[1,128]{1,0:T(1,128)} fusion(s32[8]{0:T(128)} %own_len.1), kind=kLoop, calls=%fused_computation.1 | loop fusion | bytes 544 | tf_op jit(solution)/shard_map/reshape | solution.py:722
  1.8 28.1 %gather_project.1 = (bf16[512,1024]{1,0:T(8,128)(2,1)}, bf16[8,64,256]{2,1,0:T(8,128)(2,1)}, bf16[512,256]{1,0:T(8,128)(2,1)}, bf16[512,256]{1,0:T(8,128)(2,1)},...) custom-call(bf16[512,256]{1,0:T(8,128)(2,1)} %hidden.1, bf16[3,1024,256]{2,1,0:T(8,128)(2,1)} %bitcast.7, ...), custom_call_target="tpu_custom_call" | custom-call | tf_op jit(solution)/shard_map/gather_project/pallas_call | solution.py:155
  29.9 35.0 %attend.1 = (bf16[512,256]{1,0:T(8,128)(2,1)}, bf16[8,64,256]{2,1,0:T(8,128)(2,1)}, bf16[8,64,256]{2,1,0:T(8,128)(2,1)}, bf16[3,256,1024]{2,1,0:T(8,128)(2,1)}) custom-call(bf16[8,64,256]{2,1,0:T(8,128)(2,1)} %get-tuple-element.13.q, bf16[512,256]{1,0:T(8,128)(2,1)} %get-tuple-element.14.k, bf16[512,256]{1,0:T(8,128)(2,1)} %get-tuple-element.15.v, ...), custom_call_target="tpu_custom_call" | custom-call | tf_op jit(solution)/shard_map/attend/pallas_call | solution.py:507
  64.9 0.0 copy-start.1
  65.0 0.0 copy-start.2
  65.0 34.0 %finish.1 = bf16[512,256]{1,0:T(8,128)(2,1)} custom-call(bf16[512,256]{1,0:T(8,128)(2,1)} %get-tuple-element.19.att, bf16[512,1024]{1,0:T(8,128)(2,1)} %get-tuple-element.20.x, bf16[256,1024]{1,0:T(8,128)(2,1)} %w_own.3, bf16[3,256,1024]{2,1,0:T(8,128)(2,1)} %get-tuple-element.21.w_far, bf16[1024,1024]{1,0:T(8,128)(2,1)} %w_up.1, bf16[1024,1024]{1,0:T(8,128)(2,1)} %w_down.1, ...), custom_call_target="tpu_custom_call" | custom-call | tf_op jit(solution)/shard_map/finish/pallas_call | solution.py:678
  98.9 0.0 copy-done.1
  98.9 0.0 copy-done.2
  99.0 0.0 copy-start
  99.0 0.1 pad_maximum_fusion
  99.0 1.3 %copy.14 = bf16[8,64,2,256]{3,2,1,0:T(2,128)(2,1)} copy(bf16[8,64,2,256]{3,1,0,2:T(8,128)(2,1)S(1)} %pad_maximum_fusion) | data formatting | bytes 1048576
  100.4 0.0 copy-done
  100.4 0.7 copy.16
Async XLA Ops:
  64.9 34.0 %copy-start.1 = (bf16[8,64,256]{2,1,0:T(8,128)(2,1)S(1)}, bf16[8,64,256]{2,1,0:T(8,128)(2,1)}, u32[]{:S(2)}) copy-start(bf16[8,64,256]{2,1,0:T(8,128)(2,1)} %get-tuple-element.22) | copy-start | bytes 786436
  65.0 34.0 %copy-start.2 = (bf16[8,64,256]{2,1,0:T(8,128)(2,1)S(1)}, bf16[8,64,256]{2,1,0:T(8,128)(2,1)}, u32[]{:S(2)}) copy-start(bf16[8,64,256]{2,1,0:T(8,128)(2,1)} %get-tuple-element.23) | copy-start | bytes 786436
  99.0 1.4 %copy-start = (bf16[512,256]{1,0:T(8,128)(2,1)S(1)}, bf16[512,256]{1,0:T(8,128)(2,1)}, u32[]{:S(2)}) copy-start(bf16[512,256]{1,0:T(8,128)(2,1)} %finish.1) | copy-start | bytes 786436

commit v2 on v0

v2 whole, which is shorter than its diff:
```python
import functools

import jax
import jax.numpy as jnp
from jax import lax
from jax.experimental import pallas as pl
from jax.experimental.pallas import tpu as pltpu
from jax.sharding import PartitionSpec as P

HD = 64
NEG = -1e30
EPS = 1e-05
BF = jnp.bfloat16
F32 = jnp.float32
MESH = pl.DeviceIdType.MESH
VMEM_BYTES = 60 * 2**20


def dot(a, b):
    return jnp.dot(a, b, preferred_element_type=F32)


def dot_t(a, b):
    return lax.dot_general(a, b, (((1,), (1,)), ((), ())), preferred_element_type=F32)


def iota(shape, dim):
    return lax.broadcasted_iota(jnp.int32, shape, dim)


def remote(src, dst, ssem, rsem, dev):
    return pltpu.make_async_remote_copy(
        src_ref=src, dst_ref=dst, send_sem=ssem, recv_sem=rsem, device_id=dev, device_id_type=MESH
    )


def greet(devices):
    barrier = pltpu.get_barrier_semaphore()
    for dev in devices:
        pl.semaphore_signal(barrier, inc=1, device_id=dev, device_id_type=MESH)
    pl.semaphore_wait(barrier, len(devices))


def diagonal(rows64, mask):
    return jnp.concatenate([rows64] * 4, axis=0) * mask


def fold(wide, draft):
    lane = iota((draft, wide.shape[1]), 1)
    out = wide[0:draft]
    for h in range(1, wide.shape[1] // HD):
        out = jnp.where(lane >= h * HD, wide[h * draft : (h + 1) * draft], out)
    return out


def page_part(queries, page, count, draft):
    scores = pltpu.roll(dot_t(queries, page), 1, 1)
    lane = iota(scores.shape, 1)
    valid = (lane < 2 * count) & (lax.rem(lane, 2) == 1)
    top = jnp.max(jnp.where(valid, scores, NEG), axis=1, keepdims=True)
    weights = jnp.where(valid, jnp.exp(scores - top), 0.0).astype(BF)
    total = jnp.sum(weights.astype(F32), axis=1, keepdims=True)
    return fold(dot(weights, page), draft), top, total


def spread(column, draft):
    lane = iota((draft, 128), 1)
    tiles = []
    for i in range(2):
        a = jnp.broadcast_to(column[2 * i * draft : (2 * i + 1) * draft], (draft, 128))
        b = jnp.broadcast_to(column[(2 * i + 1) * draft : (2 * i + 2) * draft], (draft, 128))
        tiles.append(jnp.where(lane < HD, a, b))
    return jnp.concatenate(tiles, axis=1)


def place(stats, column, at):
    lane = iota(stats.shape, 1)
    return jnp.where(lane == at, column, stats)


def layer_kernel(
    sizes,
    hidden,
    w_own,
    gain1,
    gain2,
    parents,
    accept,
    page_table,
    own_len,
    qkv_hbm,
    up_hbm,
    down_hbm,
    pool,
    out,
    kept_k,
    kept_v,
    weights,
    w_up,
    w_down,
    pages_v,
    load_sem,
    x_v,
    q,
    k,
    v,
    reach,
    select,
    lens_row,
    lbuf,
    far_len,
    xbuf,
    qlong,
    q_one,
    q_far,
    part_one,
    stat_one,
    part_far,
    stat_far,
    back_one,
    bstat_one,
    back_far,
    bstat_far,
    acc,
    own_stat,
    wbuf,
    att,
    abuf,
    normed_v,
    share_v,
    obuf,
    rbuf,
    second_v,
    srow,
    sbuf,
    xs,
    xr,
    vs,
    vr,
    ls,
    lr,
    q1s,
    q1r,
    qfs,
    qfr,
    p1s,
    p1r,
    t1s,
    t1r,
    pfs,
    pfr,
    tfs,
    tfr,
    ws,
    wr,
    fs,
    fr,
    as_,
    ar,
    bs,
    br,
    os_,
    or_,
    ss,
    sr,
):
    n_req, n_tp, pages, chunks = sizes
    e = lax.axis_index("req")
    t = lax.axis_index("tp")
    tokens, share = hidden.shape
    requests, draft = parents.shape
    rows = tokens // chunks
    step = rows // 2
    width = share
    full = share * n_tp
    page_len = pages_v.shape[1]
    longs = (requests + 3) // 4
    half = w_own.shape[0] // 2
    parity = lax.rem(e, 2)
    partner = (e + 1 - 2 * parity, t)
    peers = [(e, lax.rem(t + r, n_tp)) for r in range(1, n_tp)]
    right, left = peers[0], peers[2]

    def ahead(j):
        return (lax.rem(e + j, n_req), t)

    def behind(j):
        return (lax.rem(e - j + n_req, n_req), t)

    loads = [
        pltpu.make_async_copy(a, b, load_sem.at[i])
        for i, (a, b) in enumerate(
            [(qkv_hbm, weights), (pool, pages_v), (up_hbm, w_up), (down_hbm, w_down)]
        )
    ]
    for load in loads:
        load.start()

    lane_row = iota((1, 128), 1)
    line = jnp.zeros((1, 128), jnp.int32)
    for m in range(requests):
        line = jnp.where(lane_row == m, own_len[m], line)
    lens_row[...] = line

    greet(peers + [ahead(j) for j in range(1, pages)] + [behind(j) for j in range(1, pages)])

    def span_of(c):
        return pl.ds(c * rows, rows)

    def part_of(c, i):
        return pl.ds(c * rows + i * step, step)

    def len_copy(j):
        return remote(lens_row, lbuf.at[j - 1], ls.at[j - 1], lr.at[j - 1], ahead(j))

    def near(source, buf, send, recv, i, c):
        span = span_of(c)
        return remote(
            source.at[span], buf.at[2 * i, span], send.at[i, c], recv.at[i, c], (right, left)[i]
        )

    def onward(buf, send, recv, i, c):
        span = part_of(c, i)
        return remote(
            buf.at[2 * i, span], buf.at[1, span], send.at[i, c], recv.at[i, c], (right, left)[i]
        )

    def x_near(i, c):
        return near(hidden, xbuf, xs, xr, i, c)

    def x_onward(i, c):
        return onward(xbuf, vs, vr, i, c)

    def a_near(i, c):
        return near(att, abuf, as_, ar, i, c)

    def a_onward(i, c):
        return onward(abuf, bs, br, i, c)

    def far_q(j):
        return remote(qlong, q_far.at[j - 2], qfs.at[j - 2], qfr.at[j - 2], ahead(j))

    def one_q(c):
        span = pl.ds(2 * c, 2)
        return remote(q.at[span], q_one.at[span], q1s.at[c], q1r.at[c], ahead(1))

    def one_part(c):
        return remote(part_one.at[c], back_one.at[c], p1s.at[c], p1r.at[c], behind(1))

    def one_stat():
        return remote(stat_one, bstat_one, t1s, t1r, behind(1))

    def far_part(j):
        return remote(part_far.at[j - 2], back_far.at[j - 2], pfs.at[j - 2], pfr.at[j - 2], behind(j))

    def far_stat(j):
        return remote(stat_far.at[j - 2], bstat_far.at[j - 2], tfs.at[j - 2], tfr.at[j - 2], behind(j))

    def w_half(r, which):
        return wbuf.at[r - 1, pl.ds(pl.multiple_of(which * half, half), half)]

    def w_copy(r):
        return remote(
            w_own.at[pl.ds(pl.multiple_of(parity * half, half), half)],
            w_half(r, parity),
            ws.at[r - 1],
            wr.at[r - 1],
            peers[r - 1],
        )

    def w_pass(r, which):
        return remote(w_half(r, which), w_half(r, which), fs.at[r - 1], fr.at[r - 1], partner)

    def o_copy(r, c):
        s = lax.rem(t + r, n_tp)
        span = span_of(c)
        return remote(
            obuf.at[span, pl.ds(pl.multiple_of(s * share, share), share)],
            rbuf.at[r - 1, span],
            os_.at[r - 1, c],
            or_.at[r - 1, c],
            peers[r - 1],
        )

    def s_copy(r):
        return remote(srow, sbuf.at[r - 1], ss.at[r - 1], sr.at[r - 1], peers[r - 1])

    for j in range(1, pages):
        len_copy(j).start()
    for c in range(chunks):
        for i in range(2):
            x_near(i, c).start()

    per = 256 // draft
    wide = per * draft

    def ancestors(g):
        line = jnp.concatenate(
            [
                jnp.where(
                    parents[g * per + b : g * per + b + 1, :] < 0,
                    -1,
                    parents[g * per + b : g * per + b + 1, :] + b * draft,
                )
                for b in range(per)
            ],
            axis=1,
        )
        low = iota((wide, wide), 0)
        high = iota((wide, wide), 1)
        up = jnp.where((low == line) | (low == high), 1.0, 0.0)
        steps = max(1, (draft - 1).bit_length())
        for _ in range(steps):
            last = up.astype(BF)
            up = jnp.minimum(dot(last, last), 1.0)
        down = jnp.swapaxes(up, 0, 1)
        depth = jnp.sum(up, axis=0, keepdims=True) - 1.0
        hit = low == -1
        for b in range(per):
            hit = hit | (low == accept[g * per + b] + b * draft)
        chosen = jnp.sum(jnp.where(hit, down, 0.0), axis=0, keepdims=True)
        level = iota((draft, wide), 0).astype(F32)
        select[g] = jnp.where(level == depth, chosen, 0.0).astype(BF)
        for b in range(per):
            span = slice(b * draft, (b + 1) * draft)
            reach[g * per + b] = down[span, span]

    def x_arrive(c):
        for i in range(2):
            x_near(i, c).wait_recv()
            x_onward(i, c).start()

    groups = requests // per
    ancestors(0)
    for c in range(chunks // 2):
        x_arrive(c)
    for g in range(1, groups):
        ancestors(g)
    for c in range(chunks // 2, chunks):
        x_arrive(c)

    def columns_of(s):
        return pl.ds(pl.multiple_of(s * share, share), share)

    loads[0].wait()
    for c in range(chunks):
        span = span_of(c)
        x_v[span, columns_of(t)] = hidden[span]
        for r in (1, 3):
            x_v[span, columns_of(lax.rem(t - r + n_tp, n_tp))] = xbuf[r - 1, span]
        for i in range(2):
            x_onward(i, c).wait_recv()
        x_v[span, columns_of(lax.rem(t - 2 + n_tp, n_tp))] = xbuf[1, span]
        x = x_v[span]
        both = (dot(x, weights[0]) * 0.125).astype(BF)
        for i in range(rows // draft):
            q[c * rows // draft + i] = both[i * draft : (i + 1) * draft]
        one_q(c).start()
        k[span] = dot(x, weights[1]).astype(BF)
        v[span] = dot(x, weights[2]).astype(BF)

    def long_pair(length):
        first = jnp.int32(requests)
        second = jnp.int32(0)
        for m in range(requests):
            is_long = length(m) > 2 * page_len
            first = jnp.where(is_long, jnp.minimum(first, m), first)
            second = jnp.where(is_long, jnp.maximum(second, m), second)
        return jnp.minimum(first, requests - 1), second

    mine = long_pair(lambda m: own_len[m])
    for i in range(longs):
        qlong[i] = q[mine[i]]
    for j in range(pages - 1, 1, -1):
        far_q(j).start()
    for r in range(1, n_tp):
        w_copy(r).start()

    for j in range(1, pages):
        len_copy(j).wait_recv()
    lens_in = pltpu.make_async_copy(lbuf, far_len, load_sem.at[4])
    lens_in.start()

    mask = jnp.where(
        iota((4 * draft, width), 0) // draft == iota((4 * draft, width), 1) // HD, 1.0, 0.0
    ).astype(BF)

    loads[1].wait()
    lens_in.wait()

    def page_of(slot):
        return pages_v[slot].reshape(2 * page_len, width)

    stats = jnp.zeros((4 * draft, 128), F32)
    for c in range(chunks):
        one_q(c).wait_recv()
        for i in range(2):
            r = 2 * c + i
            count = far_len[0, 0, r] - page_len
            queries = diagonal(q_one[r], mask)
            part, top, total = page_part(queries, page_of(page_table[1, r]), count, draft)
            part_one[c, i * draft : (i + 1) * draft] = part.astype(BF)
            stats = place(place(stats, top, 2 * r), total, 2 * r + 1)
        one_part(c).start()
    stat_one[...] = jnp.swapaxes(stats, 0, 1)[0:16]
    one_stat().start()

    for j in range(pages - 1, 1, -1):
        pair = long_pair(lambda m: far_len[j - 1, 0, m])
        far_q(j).wait_recv()
        stats = jnp.zeros((4 * draft, 128), F32)
        for i in range(longs):
            slot = page_table[j, 0]
            count = far_len[j - 1, 0, 0]
            for m in range(1, requests):
                slot = jnp.where(pair[i] == m, page_table[j, m], slot)
                count = jnp.where(pair[i] == m, far_len[j - 1, 0, m], count)
            count = count - j * page_len
            queries = diagonal(q_far[j - 2, i], mask)
            part, top, total = page_part(queries, page_of(slot), count, draft)
            part_far[j - 2, i * draft : (i + 1) * draft] = part.astype(BF)
            stats = place(place(stats, top, 2 * i), total, 2 * i + 1)
        stat_far[j - 2] = jnp.swapaxes(stats, 0, 1)[0:8]
        far_part(j).start()
        far_stat(j).start()

    for r in range(1, n_tp):
        w_copy(r).wait_recv()
        w_pass(r, parity).start()

    def own(r):
        span = slice(r * draft, (r + 1) * draft)
        queries = diagonal(q[r], mask)
        part, top, total = page_part(queries, page_of(page_table[0, r]), own_len[r], draft)
        allowed = jnp.concatenate([reach[r]] * 4, axis=0) > 0.5
        scores = dot_t(queries, k[span])
        tree_top = jnp.max(jnp.where(allowed, scores, NEG), axis=1, keepdims=True)
        best = jnp.maximum(top, tree_top)
        weight = jnp.where(allowed, jnp.exp(scores - best), 0.0).astype(BF)
        scale = jnp.exp(top - best)
        total = total * scale + jnp.sum(weight.astype(F32), axis=1, keepdims=True)
        tree = fold(dot(weight, v[span]), draft)
        acc[r] = part * spread(scale, draft) + tree
        own_stat[r] = place(place(jnp.zeros((4 * draft, 128), F32), best, 0), total, 1)

    def long_parts():
        for j in range(pages - 1, 1, -1):
            far_stat(j).wait_recv()
            far_part(j).wait_recv()
        far_columns = jnp.swapaxes(
            jnp.concatenate(
                [bstat_far[j - 2] for j in range(2, pages)]
                + [jnp.zeros((128 - 8 * (pages - 2), 4 * draft), F32)],
                axis=0,
            ),
            0,
            1,
        )
        found = []
        for i in range(longs):
            at = [8 * (j - 2) + 2 * i for j in range(2, pages)]
            tops = [far_columns[:, a : a + 1] for a in at]
            sums = [far_columns[:, a + 1 : a + 2] for a in at]
            best = functools.reduce(jnp.maximum, tops)
            total = jnp.zeros_like(best)
            whole = jnp.zeros((draft, width), F32)
            for j in range(2, pages):
                scale = jnp.exp(tops[j - 2] - best)
                total = total + scale * sums[j - 2]
                part = back_far[j - 2, i * draft : (i + 1) * draft].astype(F32)
                whole = whole + spread(scale, draft) * part
            found.append((whole, best, total))
        return found

    def combine(c, found, one_columns):
        one_part(c).wait_recv()
        for i in range(2):
            r = 2 * c + i
            tall = (4 * draft, 1)
            later = jnp.full(tall, mine[1], jnp.int32) == r
            is_long = jnp.full(tall, own_len[r], jnp.int32) > 2 * page_len
            top_l = jnp.where(is_long, jnp.where(later, found[1][1], found[0][1]), NEG)
            total_l = jnp.where(later, found[1][2], found[0][2])
            acc_l = jnp.where(
                jnp.full((draft, width), mine[1], jnp.int32) == r, found[1][0], found[0][0]
            )
            stat = own_stat[r]
            top_o = stat[:, 0:1]
            total_o = stat[:, 1:2]
            top_1 = one_columns[:, 2 * r : 2 * r + 1]
            total_1 = one_columns[:, 2 * r + 1 : 2 * r + 2]
            best = jnp.maximum(jnp.maximum(top_o, top_1), top_l)
            s_o = jnp.exp(top_o - best)
            s_1 = jnp.exp(top_1 - best)
            s_l = jnp.exp(top_l - best)
            whole = 1.0 / (s_o * total_o + s_1 * total_1 + s_l * total_l)
            y = acc[r] * spread(s_o * whole, draft)
            y = y + back_one[c, i * draft : (i + 1) * draft].astype(F32) * spread(s_1 * whole, draft)
            y = y + acc_l * spread(s_l * whole, draft)
            att[r * draft : (r + 1) * draft] = y.astype(BF)
        for i in range(2):
            a_near(i, c).start()

    def a_arrive(c):
        for i in range(2):
            a_near(i, c).wait_recv()
            a_onward(i, c).start()

    for r in range(4):
        own(r)
    found = long_parts()
    one_stat().wait_recv()
    one_columns = jnp.swapaxes(
        jnp.concatenate([bstat_one[...], jnp.zeros((128 - 16, 4 * draft), F32)], axis=0), 0, 1
    )
    for c in range(chunks):
        combine(c, found, one_columns)
        if c > 0:
            a_arrive(c - 1)
        if c + 2 < chunks:
            own(2 * c + 4)
            own(2 * c + 5)

    for r in range(1, n_tp):
        w_pass(r, 1 - parity).wait_recv()
    loads[2].wait()
    loads[3].wait()
    order = [1, 3, 2]
    mine_cols = columns_of(t)
    for c in range(chunks):
        span = span_of(c)
        branch = dot(att[span], w_own[...])
        if c == 0:
            a_arrive(chunks - 1)
        for r in (1, 3):
            branch = branch + dot(abuf[r - 1, span], wbuf[r - 1])
        for i in range(2):
            a_onward(i, c).wait_recv()
        branch = branch + dot(abuf[1, span], wbuf[1])
        z = x_v[span].astype(F32) + branch
        center = jnp.sum(z, axis=1, keepdims=True) / full
        var = jnp.sum(z * z, axis=1, keepdims=True) / full - center * center
        normed = ((z - center) * lax.rsqrt(var + EPS) * gain1[...]).astype(BF)
        normed_v[...] = normed
        share_v[span] = normed_v[:, mine_cols]
        pre = dot(normed, w_up[...])
        inner = (0.5 * pre * (1.0 + lax.erf(pre * 0.7071067811865476))).astype(BF)
        obuf[span] = dot(inner, w_down[...]).astype(BF)
        for r in order:
            o_copy(r, c).start()

    for r in range(requests):
        span = slice(r * draft, (r + 1) * draft)
        b = r % per
        pick = select[r // per][:, b * draft : (b + 1) * draft]
        kept_k[r] = dot(pick, k[span]).astype(BF)
        kept_v[r] = dot(pick, v[span]).astype(BF)

    lane = iota((rows, 128), 1)
    stats = jnp.zeros((rows, 128), F32)
    for c in range(chunks):
        span = span_of(c)
        y = share_v[span].astype(F32) + obuf[span, mine_cols].astype(F32)
        for r in range(1, n_tp):
            o_copy(r, c).wait_recv()
            y = y + rbuf[r - 1, span].astype(F32)
        second_v[span] = y
        stats = jnp.where(lane == 2 * c, jnp.sum(y, axis=1, keepdims=True), stats)
        stats = jnp.where(lane == 2 * c + 1, jnp.sum(y * y, axis=1, keepdims=True), stats)
    total = jnp.swapaxes(stats, 0, 1)[0:8]
    srow[...] = total
    for r in order:
        s_copy(r).start()
    for r in range(1, n_tp):
        s_copy(r).wait_recv()
        total = total + sbuf[r - 1]
    columns = jnp.swapaxes(
        jnp.concatenate([total, jnp.zeros((128 - 8, rows), F32)], axis=0), 0, 1
    )
    for c in range(chunks):
        span = span_of(c)
        center = columns[:, 2 * c : 2 * c + 1] / full
        var = columns[:, 2 * c + 1 : 2 * c + 2] / full - center * center
        out[span] = ((second_v[span] - center) * lax.rsqrt(var + EPS) * gain2[:, mine_cols]).astype(BF)

    for j in range(1, pages):
        len_copy(j).wait_send()
    for j in range(2, pages):
        far_q(j).wait_send()
        far_part(j).wait_send()
        far_stat(j).wait_send()
    one_stat().wait_send()
    for c in range(chunks):
        one_q(c).wait_send()
        one_part(c).wait_send()
        for i in range(2):
            x_near(i, c).wait_send()
            x_onward(i, c).wait_send()
            a_near(i, c).wait_send()
            a_onward(i, c).wait_send()
    for r in range(1, n_tp):
        w_copy(r).wait_send()
        w_pass(r, parity).wait_send()
        s_copy(r).wait_send()
        for c in range(chunks):
            o_copy(r, c).wait_send()


def layer(
    sizes, hidden, w_own, gain1, gain2, parents, accept, page_table, own_len, w_qkv, w_up, w_down, pool
):
    n_req, n_tp, pages, chunks = sizes
    tokens, share = hidden.shape
    requests, draft = parents.shape
    full = share * n_tp
    rows = tokens // chunks
    far = pages - 2
    others = n_tp - 1
    vm = pl.BlockSpec(memory_space=pltpu.VMEM)
    sm = pl.BlockSpec(memory_space=pltpu.SMEM)
    hbm = pl.BlockSpec(memory_space=pl.ANY)
    sds = jax.ShapeDtypeStruct
    dma = pltpu.SemaphoreType.DMA
    vmem = pltpu.VMEM
    pairs = [dma(s) for s in [(2, chunks), (2, chunks), (pages - 1,), (chunks,), (far,), (chunks,)] for _ in range(2)]
    pairs += [dma, dma]
    pairs += [
        dma(s)
        for s in [(far,), (far,), (others,), (others,), (2, chunks), (2, chunks), (others, chunks), (others,)]
        for _ in range(2)
    ]
    return pl.pallas_call(
        functools.partial(layer_kernel, sizes),
        out_shape=(
            sds((tokens, share), BF),
            sds((requests, draft, share), BF),
            sds((requests, draft, share), BF),
        ),
        in_specs=[vm, vm, vm, vm, vm, sm, sm, sm, hbm, hbm, hbm, hbm],
        out_specs=(vm,) * 3,
        scratch_shapes=[
            vmem(w_qkv.shape, BF),
            vmem(w_up.shape, BF),
            vmem(w_down.shape, BF),
            vmem(pool.shape, BF),
            dma((5,)),
            vmem((tokens, full), BF),
            vmem((requests, draft, share), BF),
            vmem((tokens, share), BF),
            vmem((tokens, share), BF),
            vmem((requests, draft, draft), F32),
            vmem((requests * draft // 256, draft, 256), BF),
            vmem((1, 128), jnp.int32),
            vmem((pages - 1, 1, 128), jnp.int32),
            pltpu.SMEM((pages - 1, 1, 128), jnp.int32),
            vmem((others, tokens, share), BF),
            vmem((2, draft, share), BF),
            vmem((requests, draft, share), BF),
            vmem((far, 2, draft, share), BF),
            vmem((chunks, 2 * draft, share), BF),
            vmem((16, 4 * draft), F32),
            vmem((far, 2 * draft, share), BF),
            vmem((far, 8, 4 * draft), F32),
            vmem((chunks, 2 * draft, share), BF),
            vmem((16, 4 * draft), F32),
            vmem((far, 2 * draft, share), BF),
            vmem((far, 8, 4 * draft), F32),
            vmem((requests, draft, share), F32),
            vmem((requests, 4 * draft, 128), F32),
            vmem((others,) + w_own.shape, BF),
            vmem((tokens, share), BF),
            vmem((others, tokens, share), BF),
            vmem((rows, full), BF),
            vmem((tokens, share), BF),
            vmem((tokens, full), BF),
            vmem((others, tokens, share), BF),
            vmem((tokens, share), F32),
            vmem((8, rows), F32),
            vmem((others, 8, rows), F32),
        ]
        + pairs,
        compiler_params=pltpu.CompilerParams(
            collective_id=0, has_side_effects=True, vmem_limit_bytes=VMEM_BYTES
        ),
        name="layer",
    )(
        hidden,
        w_own,
        gain1.reshape(1, -1),
        gain2.reshape(1, -1),
        parents,
        accept,
        page_table,
        own_len,
        w_qkv,
        w_up,
        w_down,
        pool,
    )


def shards(
    sizes,
    hidden_in,
    w_qkv,
    w_out,
    first_gain,
    w_up,
    w_down,
    second_gain,
    cache_pool,
    page_table,
    cache_len,
    tree_parent,
    accept_node,
):
    layer_out, kept_k, kept_v = layer(
        sizes,
        hidden_in,
        w_out,
        first_gain,
        second_gain,
        tree_parent,
        accept_node,
        page_table,
        cache_len,
        jnp.transpose(w_qkv, (1, 0, 2)),
        w_up,
        w_down,
        cache_pool,
    )
    return layer_out, jnp.stack([kept_k, kept_v], axis=2)


def solution(mesh):
    placed = (
        P("req", "tp"),
        P(None, None, "tp"),
        P("tp", None),
        P(),
        P(None, "tp"),
        P("tp", None),
        P(),
        P("req", None, None, "tp"),
        P("req", None),
        P("req"),
        P("req", None),
        P("req"),
    )
    sizes = (mesh.shape["req"], mesh.shape["tp"], 8, 4)
    return jax.shard_map(
        functools.partial(shards, sizes),
        mesh=mesh,
        in_specs=placed,
        out_specs=(P("req", "tp"), P("req", None, None, "tp")),
        check_vma=False,
    )
```

time: 430 us -> 80.7 us (0.19); the launches traced: 425 us -> 80.6 us
  waiting for transfers between devices: 105 us -> 0 us
  matrix products: 102 us -> 0 us
  local copies, waits for them, and re-layouts: 102 us -> 2.04 us
  Pallas kernels: 0 us -> 76.8 us
  starting transfers between devices: 72.5 us -> 0 us
  other arithmetic: 19.6 us -> 1.12 us
  between operations: 15.3 us -> 0.66 us
  blocking collectives: 8.47 us -> 0 us
    dot_general x37 -> x0, matrix products: 102 us -> none  [the longest x8 64.3 us: page_rows(): jnp.einsum('rs,spcf->rpcf', picker, cache_pool, preferred_element_type=jn...]
    pallas_call x0 -> x1, Pallas kernels: none -> 76.8 us  [layer(): pl.pallas_call(functools.partial(layer_kernel, sizes), out_shape=(sds((to...]
    ppermute x41 -> x0, starting transfers between devices: 72.2 us -> none  [from_behind(): lax.ppermute(value, axis, [(i, (i + by) % size) for i in range(size)])]
    psum x1 -> x0, waiting for transfers between devices: 66.8 us -> none  [shards(): summed = lax.psum(branch, 'tp')]
    slice x25 -> x0, local copies, waits for them, and re-layouts: 32 us -> none  [the longest x16 19.2 us: rows_split(): rows[:, :, 0].reshape(requests, page_len, heads_local, HD)]
    scatter x24 -> x0, local copies, waits for them, and re-layouts: 24.4 us -> none  [the longest x12 17.2 us: spread_back(): jnp.zeros((requests,) + arrived[0].shape[1:], jnp.float32).at[long_ids]]
    reduce_scatter x1 -> x0, waiting for transfers between devices: 22.1 us -> none  [shards(): lax.psum_scatter(jnp.dot(inner, w_down, preferred_element_type=jnp.float3...]
    ppermute x41 -> x0, waiting for transfers between devices: 16.4 us -> none  [from_behind(): lax.ppermute(value, axis, [(i, (i + by) % size) for i in range(size)])]
  transfers between devices with their start and end apart: 44 -> 0, of which waited for: 6 -> 0; matrix products, arithmetic and copies ran while one was open for 42% -> 0% of each run, Pallas kernels for 0% -> 0%
where the time goes in v2:
time: 80.7 us; the launch traced here: 80.6 us
  Pallas kernels  76.8 us (95%)
  local copies, waits for them, and re-layouts  2.04 us (3%)
  other arithmetic  1.12 us (1%)
    pallas_call x1, Pallas kernels, layer(): pl.pallas_call(functools.partial(layer_kernel, sizes), out_shape=(sds((to...  76.8 us
    unnamed x4, local copies, waits for them, and re-layouts  2.04 us

profile of v2, /device:TPU:2, one launch (start us, length us, event | category | flops | bytes accessed | tf_op | source)
XLA Modules:
  0.0 80.6 jit_solution(8228410821384187409)
XLA Ops:
  0.6 76.8 %layer.1 = (bf16[512,256]{1,0:T(8,128)(2,1)}, bf16[8,64,256]{2,1,0:T(8,128)(2,1)}, bf16[8,64,256]{2,1,0:T(8,128)(2,1)}) custom-call(bf16[512,256]{1,0:T(8,128)(2,1)} %hidden.1, bf16[256,1024]{1,0:T(8,128)(2,1)} %w_own.1, f32[1,1024]{1,0:T(1,128)} %bitcast.8, f32[1,1024]{1,0:T(1,128)} %bitcast.9, s32[8,64]{1,0:T(8,128)} %parents.1, s32[8]{0:T(128)} %accept.1, ...), custom_call_target="tpu_custom_call" | custom-call | tf_op jit(solution)/shard_map/layer/pallas_call | solution.py:632
  77.4 0.0 copy-start
  77.4 1.1 %pad_maximum_fusion = bf16[8,64,2,256]{3,1,0,2:T(8,128)(2,1)S(1)} fusion(bf16[8,64,1,256]{3,1,0,2:T(8,128)(2,1)} %bitcast.7, bf16[8,64,1,256]{3,1,0,2:T(8,128)(2,1)} %bitcast.6), kind=kLoop, calls=%fused_computation | loop fusion | flops 262144 | bytes 1048576 | tf_op jit(solution)/shard_map/stack | solution.py:732
  78.6 1.3 %copy.14 = bf16[8,64,2,256]{3,2,1,0:T(2,128)(2,1)} copy(bf16[8,64,2,256]{3,1,0,2:T(8,128)(2,1)S(1)} %pad_maximum_fusion) | data formatting | bytes 1048576
  79.9 0.0 copy-done
  79.9 0.7 copy.16
Async XLA Ops:
  77.4 2.5 %copy-start = (bf16[512,256]{1,0:T(8,128)(2,1)S(1)}, bf16[512,256]{1,0:T(8,128)(2,1)}, u32[]{:S(2)}) copy-start(bf16[512,256]{1,0:T(8,128)(2,1)} %get-tuple-element.12) | copy-start | bytes 786436

commit v3 on v2

--- a/solution.py
+++ b/solution.py
@@ -93,8 +93,7 @@
     down_hbm,
     pool,
     out,
-    kept_k,
-    kept_v,
+    kept,
     weights,
     w_up,
     w_down,
@@ -131,6 +130,7 @@
     obuf,
     rbuf,
     second_v,
+    done,
     srow,
     sbuf,
     xs,
@@ -153,6 +153,8 @@
     tfr,
     ws,
     wr,
+    us,
+    ur,
     fs,
     fr,
     as_,
@@ -245,7 +247,8 @@
         return remote(q.at[span], q_one.at[span], q1s.at[c], q1r.at[c], ahead(1))
 
     def one_part(c):
-        return remote(part_one.at[c], back_one.at[c], p1s.at[c], p1r.at[c], behind(1))
+        span = pl.ds(2 * c, 2)
+        return remote(part_one.at[span], back_one.at[span], p1s.at[c], p1r.at[c], behind(1))
 
     def one_stat():
         return remote(stat_one, bstat_one, t1s, t1r, behind(1))
@@ -259,14 +262,18 @@
     def w_half(r, which):
         return wbuf.at[r - 1, pl.ds(pl.multiple_of(which * half, half), half)]
 
-    def w_copy(r):
+    def w_near(i):
         return remote(
             w_own.at[pl.ds(pl.multiple_of(parity * half, half), half)],
-            w_half(r, parity),
-            ws.at[r - 1],
-            wr.at[r - 1],
-            peers[r - 1],
+            w_half(2 * i + 1, parity),
+            ws.at[i],
+            wr.at[i],
+            (right, left)[i],
         )
+
+    def w_onward(i):
+        span = pl.ds(pl.multiple_of(parity * half + i * (half // 2), half // 2), half // 2)
+        return remote(wbuf.at[2 * i, span], wbuf.at[1, span], us.at[i], ur.at[i], (right, left)[i])
 
     def w_pass(r, which):
         return remote(w_half(r, which), w_half(r, which), fs.at[r - 1], fr.at[r - 1], partner)
@@ -342,22 +349,25 @@
     def columns_of(s):
         return pl.ds(pl.multiple_of(s * share, share), share)
 
+    def put_x(c, s, value):
+        x_v[2 * c : 2 * c + 2, :, columns_of(s)] = value.reshape(2, draft, share)
+
     loads[0].wait()
     for c in range(chunks):
         span = span_of(c)
-        x_v[span, columns_of(t)] = hidden[span]
+        put_x(c, t, hidden[span])
         for r in (1, 3):
-            x_v[span, columns_of(lax.rem(t - r + n_tp, n_tp))] = xbuf[r - 1, span]
+            put_x(c, lax.rem(t - r + n_tp, n_tp), xbuf[r - 1, span])
         for i in range(2):
             x_onward(i, c).wait_recv()
-        x_v[span, columns_of(lax.rem(t - 2 + n_tp, n_tp))] = xbuf[1, span]
-        x = x_v[span]
+        put_x(c, lax.rem(t - 2 + n_tp, n_tp), xbuf[1, span])
+        x = x_v[2 * c : 2 * c + 2].reshape(rows, full)
         both = (dot(x, weights[0]) * 0.125).astype(BF)
         for i in range(rows // draft):
             q[c * rows // draft + i] = both[i * draft : (i + 1) * draft]
         one_q(c).start()
-        k[span] = dot(x, weights[1]).astype(BF)
-        v[span] = dot(x, weights[2]).astype(BF)
+        k[2 * c : 2 * c + 2] = dot(x, weights[1]).astype(BF).reshape(2, draft, width)
+        v[2 * c : 2 * c + 2] = dot(x, weights[2]).astype(BF).reshape(2, draft, width)
 
     def long_pair(length):
         first = jnp.int32(requests)
@@ -369,12 +379,25 @@
         return jnp.minimum(first, requests - 1), second
 
     mine = long_pair(lambda m: own_len[m])
+    shorts = requests - longs
+    short = [jnp.where(own_len[m] <= 2 * page_len, 1, 0) for m in range(requests)]
+    before = [jnp.int32(0)]
+    for m in range(requests - 1):
+        before.append(before[m] + short[m])
+    work = []
+    for i in range(shorts):
+        found = jnp.int32(0)
+        for m in range(requests):
+            found = jnp.where((short[m] == 1) & (before[m] == i), m, found)
+        work.append(found)
+    work += [mine[0], mine[1]]
+    place_of = [jnp.where(short[m] == 1, before[m], shorts + m - before[m]) for m in range(requests)]
     for i in range(longs):
         qlong[i] = q[mine[i]]
     for j in range(pages - 1, 1, -1):
         far_q(j).start()
-    for r in range(1, n_tp):
-        w_copy(r).start()
+    for i in range(2):
+        w_near(i).start()
 
     for j in range(1, pages):
         len_copy(j).wait_recv()
@@ -399,13 +422,15 @@
             count = far_len[0, 0, r] - page_len
             queries = diagonal(q_one[r], mask)
             part, top, total = page_part(queries, page_of(page_table[1, r]), count, draft)
-            part_one[c, i * draft : (i + 1) * draft] = part.astype(BF)
+            part_one[r] = part.astype(BF)
             stats = place(place(stats, top, 2 * r), total, 2 * r + 1)
         one_part(c).start()
-    stat_one[...] = jnp.swapaxes(stats, 0, 1)[0:16]
+    turned = jnp.swapaxes(stats, 0, 1)
+    for r in range(requests):
+        stat_one[r] = turned[2 * r : 2 * r + 2]
     one_stat().start()
 
-    for j in range(pages - 1, 1, -1):
+    def far_pages(j):
         pair = long_pair(lambda m: far_len[j - 1, 0, m])
         far_q(j).wait_recv()
         stats = jnp.zeros((4 * draft, 128), F32)
@@ -424,24 +449,20 @@
         far_part(j).start()
         far_stat(j).start()
 
-    for r in range(1, n_tp):
-        w_copy(r).wait_recv()
-        w_pass(r, parity).start()
-
-    def own(r):
-        span = slice(r * draft, (r + 1) * draft)
+    def own(p):
+        r = work[p]
         queries = diagonal(q[r], mask)
         part, top, total = page_part(queries, page_of(page_table[0, r]), own_len[r], draft)
         allowed = jnp.concatenate([reach[r]] * 4, axis=0) > 0.5
-        scores = dot_t(queries, k[span])
+        scores = dot_t(queries, k[r])
         tree_top = jnp.max(jnp.where(allowed, scores, NEG), axis=1, keepdims=True)
         best = jnp.maximum(top, tree_top)
         weight = jnp.where(allowed, jnp.exp(scores - best), 0.0).astype(BF)
         scale = jnp.exp(top - best)
         total = total * scale + jnp.sum(weight.astype(F32), axis=1, keepdims=True)
-        tree = fold(dot(weight, v[span]), draft)
-        acc[r] = part * spread(scale, draft) + tree
-        own_stat[r] = place(place(jnp.zeros((4 * draft, 128), F32), best, 0), total, 1)
+        tree = fold(dot(weight, v[r]), draft)
+        acc[p] = part * spread(scale, draft) + tree
+        own_stat[p] = place(place(jnp.zeros((4 * draft, 128), F32), best, 0), total, 1)
 
     def long_parts():
         for j in range(pages - 1, 1, -1):
@@ -472,32 +493,30 @@
             found.append((whole, best, total))
         return found
 
-    def combine(c, found, one_columns):
-        one_part(c).wait_recv()
+    def combine(c, one_columns, found=None):
         for i in range(2):
-            r = 2 * c + i
-            tall = (4 * draft, 1)
-            later = jnp.full(tall, mine[1], jnp.int32) == r
-            is_long = jnp.full(tall, own_len[r], jnp.int32) > 2 * page_len
-            top_l = jnp.where(is_long, jnp.where(later, found[1][1], found[0][1]), NEG)
-            total_l = jnp.where(later, found[1][2], found[0][2])
-            acc_l = jnp.where(
-                jnp.full((draft, width), mine[1], jnp.int32) == r, found[1][0], found[0][0]
-            )
-            stat = own_stat[r]
+            p = 2 * c + i
+            stat = own_stat[p]
             top_o = stat[:, 0:1]
             total_o = stat[:, 1:2]
-            top_1 = one_columns[:, 2 * r : 2 * r + 1]
-            total_1 = one_columns[:, 2 * r + 1 : 2 * r + 2]
-            best = jnp.maximum(jnp.maximum(top_o, top_1), top_l)
+            top_1 = one_columns[:, 2 * p : 2 * p + 1]
+            total_1 = one_columns[:, 2 * p + 1 : 2 * p + 2]
+            best = jnp.maximum(top_o, top_1)
+            if found is not None:
+                acc_l, top_l, total_l = found[i]
+                best = jnp.maximum(best, top_l)
             s_o = jnp.exp(top_o - best)
             s_1 = jnp.exp(top_1 - best)
-            s_l = jnp.exp(top_l - best)
-            whole = 1.0 / (s_o * total_o + s_1 * total_1 + s_l * total_l)
-            y = acc[r] * spread(s_o * whole, draft)
-            y = y + back_one[c, i * draft : (i + 1) * draft].astype(F32) * spread(s_1 * whole, draft)
-            y = y + acc_l * spread(s_l * whole, draft)
-            att[r * draft : (r + 1) * draft] = y.astype(BF)
+            whole = s_o * total_o + s_1 * total_1
+            if found is not None:
+                s_l = jnp.exp(top_l - best)
+                whole = whole + s_l * total_l
+            whole = 1.0 / whole
+            y = acc[p] * spread(s_o * whole, draft)
+            y = y + back_one[work[p]].astype(F32) * spread(s_1 * whole, draft)
+            if found is not None:
+                y = y + acc_l * spread(s_l * whole, draft)
+            att[p * draft : (p + 1) * draft] = y.astype(BF)
         for i in range(2):
             a_near(i, c).start()
 
@@ -506,20 +525,40 @@
             a_near(i, c).wait_recv()
             a_onward(i, c).start()
 
-    for r in range(4):
-        own(r)
-    found = long_parts()
+    for i in range(2):
+        w_near(i).wait_recv()
+        w_onward(i).start()
+    for p in range(4):
+        own(p)
     one_stat().wait_recv()
+    for c in range(chunks):
+        one_part(c).wait_recv()
     one_columns = jnp.swapaxes(
-        jnp.concatenate([bstat_one[...], jnp.zeros((128 - 16, 4 * draft), F32)], axis=0), 0, 1
+        jnp.concatenate(
+            [bstat_one[work[p]] for p in range(requests)] + [jnp.zeros((128 - 16, 4 * draft), F32)],
+            axis=0,
+        ),
+        0,
+        1,
     )
-    for c in range(chunks):
-        combine(c, found, one_columns)
-        if c > 0:
-            a_arrive(c - 1)
-        if c + 2 < chunks:
-            own(2 * c + 4)
-            own(2 * c + 5)
+    combine(0, one_columns)
+    combine(1, one_columns)
+
+    for i in range(2):
+        w_onward(i).wait_recv()
+    for r in range(1, n_tp):
+        w_pass(r, parity).start()
+    for j in range(pages - 1, 1, -1):
+        far_pages(j)
+        if j == pages - 2:
+            a_arrive(0)
+        if j == pages - 3:
+            a_arrive(1)
+    own(4)
+    own(5)
+    combine(2, one_columns)
+    own(6)
+    own(7)
 
     for r in range(1, n_tp):
         w_pass(r, 1 - parity).wait_recv()
@@ -529,15 +568,20 @@
     mine_cols = columns_of(t)
     for c in range(chunks):
         span = span_of(c)
+        if c == 1:
+            a_arrive(2)
+        if c == 2:
+            combine(3, one_columns, long_parts())
+        if c == 3:
+            a_arrive(3)
         branch = dot(att[span], w_own[...])
-        if c == 0:
-            a_arrive(chunks - 1)
         for r in (1, 3):
             branch = branch + dot(abuf[r - 1, span], wbuf[r - 1])
         for i in range(2):
             a_onward(i, c).wait_recv()
         branch = branch + dot(abuf[1, span], wbuf[1])
-        z = x_v[span].astype(F32) + branch
+        x = jnp.concatenate([x_v[work[2 * c]], x_v[work[2 * c + 1]]], axis=0)
+        z = x.astype(F32) + branch
         center = jnp.sum(z, axis=1, keepdims=True) / full
         var = jnp.sum(z * z, axis=1, keepdims=True) / full - center * center
         normed = ((z - center) * lax.rsqrt(var + EPS) * gain1[...]).astype(BF)
@@ -550,11 +594,10 @@
             o_copy(r, c).start()
 
     for r in range(requests):
-        span = slice(r * draft, (r + 1) * draft)
         b = r % per
         pick = select[r // per][:, b * draft : (b + 1) * draft]
-        kept_k[r] = dot(pick, k[span]).astype(BF)
-        kept_v[r] = dot(pick, v[span]).astype(BF)
+        kept[r, :, 0:width] = dot(pick, k[r]).astype(BF)
+        kept[r, :, width : 2 * width] = dot(pick, v[r]).astype(BF)
 
     lane = iota((rows, 128), 1)
     stats = jnp.zeros((rows, 128), F32)
@@ -581,7 +624,10 @@
         span = span_of(c)
         center = columns[:, 2 * c : 2 * c + 1] / full
         var = columns[:, 2 * c + 1 : 2 * c + 2] / full - center * center
-        out[span] = ((second_v[span] - center) * lax.rsqrt(var + EPS) * gain2[:, mine_cols]).astype(BF)
+        y = (second_v[span] - center) * lax.rsqrt(var + EPS) * gain2[:, mine_cols]
+        done[2 * c : 2 * c + 2] = y.astype(BF).reshape(2, draft, share)
+    for r in range(requests):
+        out[r * draft : (r + 1) * draft] = done[place_of[r]]
 
     for j in range(1, pages):
         len_copy(j).wait_send()
@@ -598,8 +644,10 @@
             x_onward(i, c).wait_send()
             a_near(i, c).wait_send()
             a_onward(i, c).wait_send()
+    for i in range(2):
+        w_near(i).wait_send()
+        w_onward(i).wait_send()
     for r in range(1, n_tp):
-        w_copy(r).wait_send()
         w_pass(r, parity).wait_send()
         s_copy(r).wait_send()
         for c in range(chunks):
@@ -626,28 +674,27 @@
     pairs += [dma, dma]
     pairs += [
         dma(s)
-        for s in [(far,), (far,), (others,), (others,), (2, chunks), (2, chunks), (others, chunks), (others,)]
+        for s in [(far,), (far,), (2,), (2,), (others,), (2, chunks), (2, chunks), (others, chunks), (others,)]
         for _ in range(2)
     ]
     return pl.pallas_call(
         functools.partial(layer_kernel, sizes),
         out_shape=(
             sds((tokens, share), BF),
-            sds((requests, draft, share), BF),
-            sds((requests, draft, share), BF),
+            sds((requests, draft, 2 * share), BF),
         ),
         in_specs=[vm, vm, vm, vm, vm, sm, sm, sm, hbm, hbm, hbm, hbm],
-        out_specs=(vm,) * 3,
+        out_specs=(vm,) * 2,
         scratch_shapes=[
             vmem(w_qkv.shape, BF),
             vmem(w_up.shape, BF),
             vmem(w_down.shape, BF),
             vmem(pool.shape, BF),
             dma((5,)),
-            vmem((tokens, full), BF),
+            vmem((requests, draft, full), BF),
             vmem((requests, draft, share), BF),
-            vmem((tokens, share), BF),
-            vmem((tokens, share), BF),
+            vmem((requests, draft, share), BF),
+            vmem((requests, draft, share), BF),
             vmem((requests, draft, draft), F32),
             vmem((requests * draft // 256, draft, 256), BF),
             vmem((1, 128), jnp.int32),
@@ -657,12 +704,12 @@
             vmem((2, draft, share), BF),
             vmem((requests, draft, share), BF),
             vmem((far, 2, draft, share), BF),
-            vmem((chunks, 2 * draft, share), BF),
-            vmem((16, 4 * draft), F32),
+            vmem((requests, draft, share), BF),
+            vmem((requests, 2, 4 * draft), F32),
             vmem((far, 2 * draft, share), BF),
             vmem((far, 8, 4 * draft), F32),
-            vmem((chunks, 2 * draft, share), BF),
-            vmem((16, 4 * draft), F32),
+            vmem((requests, draft, share), BF),
+            vmem((requests, 2, 4 * draft), F32),
             vmem((far, 2 * draft, share), BF),
             vmem((far, 8, 4 * draft), F32),
             vmem((requests, draft, share), F32),
@@ -675,6 +722,7 @@
             vmem((tokens, full), BF),
             vmem((others, tokens, share), BF),
             vmem((tokens, share), F32),
+            vmem((requests, draft, share), BF),
             vmem((8, rows), F32),
             vmem((others, 8, rows), F32),
         ]
@@ -714,7 +762,7 @@
     tree_parent,
     accept_node,
 ):
-    layer_out, kept_k, kept_v = layer(
+    layer_out, kept = layer(
         sizes,
         hidden_in,
         w_out,
@@ -729,7 +777,8 @@
         w_down,
         cache_pool,
     )
-    return layer_out, jnp.stack([kept_k, kept_v], axis=2)
+    requests, draft = tree_parent.shape
+    return layer_out, kept.reshape(requests, draft, 2, -1)
 
 
 def solution(mesh):

time: 80.7 us -> 78.7 us (0.975)
  Pallas kernels: 76.8 us -> 74.2 us
  local copies, waits for them, and re-layouts: 2.04 us -> 3.63 us
  other arithmetic: 1.12 us -> 0 us
    pallas_call x1, Pallas kernels: 76.8 us -> 74.2 us  [layer(): pl.pallas_call(functools.partial(layer_kernel, sizes), out_shape=(sds((to...]
    reshape x0 -> x1, local copies, waits for them, and re-layouts: none -> 1.96 us  [shards(): return (layer_out, kept.reshape(requests, draft, 2, -1))]
    another operation x1 -> x0, other arithmetic: 1.12 us -> none  [shards(): return (layer_out, jnp.stack([kept_k, kept_v], axis=2))]
    unnamed x4 -> x1, local copies, waits for them, and re-layouts: 2.04 us -> 1.67 us
where the time goes in v3:
time: 78.7 us; the launch traced here: 78.5 us
  Pallas kernels  74.2 us (94%)
  local copies, waits for them, and re-layouts  3.63 us (5%)
    pallas_call x1, Pallas kernels, layer(): pl.pallas_call(functools.partial(layer_kernel, sizes), out_shape=(sds((to...  74.2 us
    reshape x1, local copies, waits for them, and re-layouts, shards(): return (layer_out, kept.reshape(requests, draft, 2, -1))  1.96 us
    unnamed x1, local copies, waits for them, and re-layouts  1.67 us

profile of v3, /device:TPU:2, one launch (start us, length us, event | category | flops | bytes accessed | tf_op | source)
XLA Modules:
  0.0 78.5 jit_solution(15355210341704671970)
XLA Ops:
  0.6 74.2 %layer.1 = (bf16[512,256]{1,0:T(8,128)(2,1)}, bf16[8,64,512]{2,1,0:T(8,128)(2,1)}) custom-call(bf16[512,256]{1,0:T(8,128)(2,1)} %hidden.1, bf16[256,1024]{1,0:T(8,128)(2,1)} %w_own.1, f32[1,1024]{1,0:T(1,128)} %bitcast.4, f32[1,1024]{1,0:T(1,128)} %bitcast.5, s32[8,64]{1,0:T(8,128)} %parents.1, s32[8]{0:T(128)} %accept.1, s32[8,8]{1,0:T(8,128)} %page_table.1, ...), custom_call_target="tpu_custom_call" | custom-call | tf_op jit(solution)/shard_map/layer/pallas_call | solution.py:680
  74.9 2.0 %reshape.15 = bf16[8,64,2,256]{3,2,1,0:T(2,128)(2,1)} reshape(bf16[8,64,512]{2,1,0:T(8,128)(2,1)} %get-tuple-element.5) | data formatting | bytes 1048576 | tf_op jit(solution)/shard_map/reshape | solution.py:781
  76.8 1.7 %copy.15 = bf16[512,256]{1,0:T(8,128)(2,1)} copy(bf16[512,256]{1,0:T(8,128)(2,1)} %get-tuple-element.8) | data formatting | bytes 524288

commit v4 on v3

--- a/solution.py
+++ b/solution.py
@@ -54,13 +54,17 @@
 
 
 def page_part(queries, page, count, draft):
-    scores = pltpu.roll(dot_t(queries, page), 1, 1)
-    lane = iota(scores.shape, 1)
-    valid = (lane < 2 * count) & (lax.rem(lane, 2) == 1)
+    n = page.shape[0] // 2
+    row = iota((2 * n, 2 * n), 0)
+    wanted = jnp.where(row < n, 2 * row, 2 * (row - n) + 1)
+    pick = jnp.where(iota((2 * n, 2 * n), 1) == wanted, 1.0, 0.0).astype(BF)
+    both = dot(pick, page).astype(BF)
+    scores = dot_t(queries, both[:n])
+    valid = iota(scores.shape, 1) < count
     top = jnp.max(jnp.where(valid, scores, NEG), axis=1, keepdims=True)
     weights = jnp.where(valid, jnp.exp(scores - top), 0.0).astype(BF)
     total = jnp.sum(weights.astype(F32), axis=1, keepdims=True)
-    return fold(dot(weights, page), draft), top, total
+    return fold(dot(weights, both[n:]), draft), top, total
 
 
 def spread(column, draft):

time: 78.7 us -> 77.6 us (0.986)
  Pallas kernels: 74.2 us -> 73.2 us
    pallas_call x1, Pallas kernels: 74.2 us -> 73.2 us  [layer(): pl.pallas_call(functools.partial(layer_kernel, sizes), out_shape=(sds((to...]
where the time goes in v4:
time: 77.6 us; the launch traced here: 77.4 us
  Pallas kernels  73.2 us (94%)
  local copies, waits for them, and re-layouts  3.63 us (5%)
    pallas_call x1, Pallas kernels, layer(): pl.pallas_call(functools.partial(layer_kernel, sizes), out_shape=(sds((to...  73.2 us
    reshape x1, local copies, waits for them, and re-layouts, shards(): return (layer_out, kept.reshape(requests, draft, 2, -1))  1.96 us
    unnamed x1, local copies, waits for them, and re-layouts  1.67 us

profile of v4, /device:TPU:2, one launch (start us, length us, event | category | flops | bytes accessed | tf_op | source)
XLA Modules:
  0.0 77.4 jit_solution(12605388715222223587)
XLA Ops:
  0.6 73.2 %layer.1 = (bf16[512,256]{1,0:T(8,128)(2,1)}, bf16[8,64,512]{2,1,0:T(8,128)(2,1)}) custom-call(bf16[512,256]{1,0:T(8,128)(2,1)} %hidden.1, bf16[256,1024]{1,0:T(8,128)(2,1)} %w_own.1, f32[1,1024]{1,0:T(1,128)} %bitcast.4, f32[1,1024]{1,0:T(1,128)} %bitcast.5, s32[8,64]{1,0:T(8,128)} %parents.1, s32[8]{0:T(128)} %accept.1, s32[8,8]{1,0:T(8,128)} %page_table.1, ...), custom_call_target="tpu_custom_call" | custom-call | tf_op jit(solution)/shard_map/layer/pallas_call | solution.py:684
  73.8 2.0 %reshape.15 = bf16[8,64,2,256]{3,2,1,0:T(2,128)(2,1)} reshape(bf16[8,64,512]{2,1,0:T(8,128)(2,1)} %get-tuple-element.5) | data formatting | bytes 1048576 | tf_op jit(solution)/shard_map/reshape | solution.py:785
  75.8 1.7 %copy.15 = bf16[512,256]{1,0:T(8,128)(2,1)} copy(bf16[512,256]{1,0:T(8,128)(2,1)} %get-tuple-element.8) | data formatting | bytes 524288
